TPU v7x, 32 devices: a whole 2x2x4 slice. The times are simulated.
32 devices in a mesh: rep: 16 (over z, x, core), shard: 2 (over y).
Axes of the slice: x: 2, y: 2, z: 4, core: 2. Of those that a mesh axis runs over, the one named last changes fastest.
Arguments:
- tokens: bfloat16 [2, 12288, 768], P(None, ('rep', 'shard')), may hold values from -6 to 6
- cotangent: bfloat16 [2, 12288, 768], P(None, ('rep', 'shard')), may hold values from -6 to 6
- seq_lengths: int32 [2, 16, 2], P(None, 'rep'), may hold values from 0 to 768, as said below
- w_query: bfloat16 [768, 768], P('shard'), may hold values from -0.21875 to 0.21875
- b_query: bfloat16 [768], P('shard'), may hold values from -1.5 to 1.5
- w_key: bfloat16 [768, 768], P('shard'), may hold values from -0.21875 to 0.21875
- w_value: bfloat16 [768, 768], P('shard'), may hold values from -0.21875 to 0.21875
- b_value: bfloat16 [768], P('shard'), may hold values from -0.5 to 0.5
- w_attn: bfloat16 [768, 768], P('shard'), may hold values from -3 to 3
- b_attn: bfloat16 [768], P('shard'), may hold values from -1 to 1
- norm_gain: bfloat16 [768], P('shard'), may hold values from 0.5 to 1.5
- norm_bias: bfloat16 [768], P('shard'), may hold values from -1 to 1
- w_up: bfloat16 [768, 3072], P('shard'), may hold values from -0.21875 to 0.21875
- b_up: bfloat16 [3072], P('shard'), may hold values from -1.5 to 1.5
- w_down: bfloat16 [3072, 768], P('shard'), may hold values from -0.109375 to 0.109375
- b_down: bfloat16 [768], P('shard'), may hold values from -1 to 1
- out_gain: bfloat16 [768], P('shard'), may hold values from 0.5 to 1.5
- out_bias: bfloat16 [768], P('shard'), may hold values from -1 to 1
Outputs:
- layer_out: bfloat16 [2, 12288, 768], P(None, ('rep', 'shard'))
- tokens_grad: bfloat16 [2, 12288, 768], P(None, ('rep', 'shard'))
- grad_w_query: float32 [768, 768], P('shard')
- grad_b_query: float32 [768], P('shard')
- grad_w_key: float32 [768, 768], P('shard')
- grad_w_value: float32 [768, 768], P('shard')
- grad_b_value: float32 [768], P('shard')
- grad_w_attn: float32 [768, 768], P('shard')
- grad_b_attn: float32 [768], P('shard')
- grad_norm_gain: float32 [768], P('shard')
- grad_norm_bias: float32 [768], P('shard')
- grad_w_up: float32 [768, 3072], P('shard')
- grad_b_up: float32 [3072], P('shard')
- grad_w_down: float32 [3072, 768], P('shard')
- grad_b_down: float32 [768], P('shard')
- grad_out_gain: float32 [768], P('shard')
- grad_out_bias: float32 [768], P('shard')
Inputs may be any that keep to these rules, and one draw needn't show every extreme that they name: `seq_lengths`: each row gives the lengths of 1 sequence in their order in the group, exactly one sequence of 768 tokens filling the group with a padding length of 0 (1024 exceeds the group); each row sums to 768.
All inputs are finite; a program needn't handle non-finite values.
Results may differ from a plain program's by a relative error of at most 0.02.
Values may be sent and summed in bfloat16 or wider, within the bound.
A program may use at most 192 MiB of HBM per device.

v0:
```python
import jax
import jax.numpy as jnp
from jax import lax
from jax.sharding import PartitionSpec as P

D = 768
H = 12
DH = 64


EPS = 1e-12
NEG = -1e30


def outer_rows(left, right):
    return lax.dot_general(
        left, right, (((0,), (0,)), ((), ())), preferred_element_type=jnp.float32
    )


def back_rows(left, right):
    return lax.dot_general(
        left, right, (((1,), (1,)), ((), ())), preferred_element_type=jnp.float32
    )


def segment_ids(row, count):
    bounds = jnp.cumsum(row[:-1])
    places = jnp.arange(count, dtype=jnp.int32)
    return jnp.sum((places[:, None] >= bounds[None, :]).astype(jnp.int32), axis=1)


def normalize(rows, gain, bias):
    mean = jnp.mean(rows, axis=-1, keepdims=True)
    centered = rows - mean
    inverse = lax.rsqrt(jnp.mean(centered * centered, axis=-1, keepdims=True) + EPS)
    normed = centered * inverse
    return (normed * gain + bias, normed, inverse)


def norm_back(grad, normed, inverse, gain):
    scaled = grad * gain
    first = jnp.mean(scaled, axis=-1, keepdims=True)
    second = jnp.mean(scaled * normed, axis=-1, keepdims=True)
    return inverse * (scaled - first - normed * second)


def gelu_slope(pre):
    lower = 0.5 * (1.0 + lax.erf(pre * 0.7071067811865476))
    density = jnp.exp(-0.5 * pre * pre) * 0.3989422804014327
    return lower + pre * density


def split_heads(rows):
    return rows.reshape(rows.shape[0], H, DH).transpose(1, 0, 2)


def join_heads(stack):
    return stack.transpose(1, 0, 2).reshape(stack.shape[1], H * DH)


def micro_step(tokens_in, slope_in, row, full, index, count):
    (
        w_query,
        b_query,
        w_key,
        w_value,
        b_value,
        w_attn,
        b_attn,
        norm_gain,
        norm_bias,
        w_up,
        b_up,
        w_down,
        b_down,
        out_gain,
        out_bias,
    ) = full
    f32 = jnp.float32
    low_type = jnp.bfloat16
    slots = tokens_in.shape[0]
    group = slots * count
    scale = DH ** (-0.5)
    nseq = row.shape[0] - 1
    key_ids = segment_ids(row, group)
    query_ids = lax.dynamic_slice_in_dim(key_ids, index * slots, slots)
    valid = (query_ids < nseq).astype(f32)
    mask = query_ids[:, None] == key_ids[None, :]
    query = (jnp.dot(tokens_in, w_query, preferred_element_type=f32) + b_query.astype(f32)).astype(
        low_type
    )
    keys = jnp.dot(tokens_in, w_key, preferred_element_type=f32).astype(low_type)
    values = (jnp.dot(tokens_in, w_value, preferred_element_type=f32) + b_value.astype(f32)).astype(
        low_type
    )
    all_keys, all_values = (
        lax.all_gather(keys, "shard", axis=0, tiled=True),
        lax.all_gather(values, "shard", axis=0, tiled=True),
    )
    head_query = split_heads(query)
    head_keys = split_heads(all_keys)
    head_values = split_heads(all_values)

    def head_forward(parts):
        one_query, one_keys, one_values = parts
        scores = jnp.where(mask, back_rows(one_query, one_keys) * scale, NEG)
        top = jnp.max(scores, axis=-1, keepdims=True)
        expo = jnp.exp(scores - top)
        total = jnp.sum(expo, axis=-1, keepdims=True)
        probs = expo / total
        mixed = jnp.dot(probs.astype(low_type), one_values, preferred_element_type=f32)
        return (mixed, (top + jnp.log(total))[:, 0])

    mixed, log_totals = lax.map(head_forward, (head_query, head_keys, head_values))
    attn = join_heads(mixed).astype(low_type)
    projected = jnp.dot(attn, w_attn, preferred_element_type=f32) + b_attn.astype(f32)
    hidden, normed_one, inverse_one = normalize(
        tokens_in.astype(f32) + projected, norm_gain.astype(f32), norm_bias.astype(f32)
    )
    hidden_low = hidden.astype(low_type)
    pre = jnp.dot(hidden_low, w_up, preferred_element_type=f32) + b_up.astype(f32)
    active = jax.nn.gelu(pre, approximate=False).astype(low_type)
    branch = jnp.dot(active, w_down, preferred_element_type=f32) + b_down.astype(f32)
    layer, normed_two, inverse_two = normalize(
        hidden + branch, out_gain.astype(f32), out_bias.astype(f32)
    )
    grad_out = slope_in.astype(f32) * valid[:, None]
    grad_out_gain = jnp.sum(grad_out * normed_two, axis=0)
    grad_out_bias = jnp.sum(grad_out, axis=0)
    grad_second = norm_back(grad_out, normed_two, inverse_two, out_gain.astype(f32))
    grad_branch = grad_second.astype(low_type)
    grad_b_down = jnp.sum(grad_branch.astype(f32), axis=0)
    grad_w_down = outer_rows(active, grad_branch)
    grad_pre = (back_rows(grad_branch, w_down) * gelu_slope(pre)).astype(low_type)
    grad_b_up = jnp.sum(grad_pre.astype(f32), axis=0)
    grad_w_up = outer_rows(hidden_low, grad_pre)
    grad_hidden = back_rows(grad_pre, w_up) + grad_second
    grad_norm_gain = jnp.sum(grad_hidden * normed_one, axis=0)
    grad_norm_bias = jnp.sum(grad_hidden, axis=0)
    grad_first = norm_back(grad_hidden, normed_one, inverse_one, norm_gain.astype(f32))
    grad_proj = grad_first.astype(low_type)
    grad_b_attn = jnp.sum(grad_proj.astype(f32), axis=0)
    grad_w_attn = outer_rows(attn, grad_proj)
    grad_attn = back_rows(grad_proj, w_attn).astype(low_type)
    head_grads = split_heads(grad_attn)

    def head_backward(parts):
        one_query, one_keys, one_values, one_grad, one_total = parts
        scores = back_rows(one_query, one_keys) * scale
        probs = jnp.where(mask, jnp.exp(scores - one_total[:, None]), 0.0)
        prob_grad = back_rows(one_grad, one_values)
        inner = jnp.sum(probs * prob_grad, axis=-1, keepdims=True)
        score_grad = (probs * (prob_grad - inner)).astype(low_type)
        query_grad = jnp.dot(score_grad, one_keys, preferred_element_type=f32) * scale
        keys_grad = outer_rows(score_grad, one_query) * scale
        values_grad = outer_rows(probs.astype(low_type), one_grad)
        return (query_grad, keys_grad, values_grad)

    query_grads, keys_grads, values_grads = lax.map(
        head_backward, (head_query, head_keys, head_values, head_grads, log_totals)
    )
    grad_query = join_heads(query_grads).astype(low_type)
    key_terms = jnp.concatenate([join_heads(keys_grads), join_heads(values_grads)], axis=1)
    own_terms = lax.psum_scatter(
        key_terms.astype(jnp.bfloat16), "shard", scatter_dimension=0, tiled=True
    ).astype(jnp.float32)
    grad_keys = own_terms[:, :D].astype(low_type)
    grad_values = own_terms[:, D:].astype(low_type)
    grad_b_query = jnp.sum(grad_query.astype(f32), axis=0)
    grad_b_value = jnp.sum(grad_values.astype(f32), axis=0)
    grad_w_query = outer_rows(tokens_in, grad_query)
    grad_w_key = outer_rows(tokens_in, grad_keys)
    grad_w_value = outer_rows(tokens_in, grad_values)
    tokens_back = (
        grad_first
        + back_rows(grad_query, w_query)
        + back_rows(grad_keys, w_key)
        + back_rows(grad_values, w_value)
    )
    local = (
        grad_w_query,
        grad_b_query,
        grad_w_key,
        grad_w_value,
        grad_b_value,
        grad_w_attn,
        grad_b_attn,
        grad_norm_gain,
        grad_norm_bias,
        grad_w_up,
        grad_b_up,
        grad_w_down,
        grad_b_down,
        grad_out_gain,
        grad_out_bias,
    )
    return (layer.astype(low_type), tokens_back.astype(low_type), local)


def body(
    tokens,
    cotangent,
    seq_lengths,
    w_query,
    b_query,
    w_key,
    w_value,
    b_value,
    w_attn,
    b_attn,
    norm_gain,
    norm_bias,
    w_up,
    b_up,
    w_down,
    b_down,
    out_gain,
    out_bias,
):
    index = lax.axis_index("shard")
    count = lax.axis_size("shard")
    layers = []
    inputs_back = []
    totals = None
    for micro in range(tokens.shape[0]):
        full = (
            lax.all_gather(w_query, "shard", axis=0, tiled=True),
            lax.all_gather(b_query, "shard", axis=0, tiled=True),
            lax.all_gather(w_key, "shard", axis=0, tiled=True),
            lax.all_gather(w_value, "shard", axis=0, tiled=True),
            lax.all_gather(b_value, "shard", axis=0, tiled=True),
            lax.all_gather(w_attn, "shard", axis=0, tiled=True),
            lax.all_gather(b_attn, "shard", axis=0, tiled=True),
            lax.all_gather(norm_gain, "shard", axis=0, tiled=True),
            lax.all_gather(norm_bias, "shard", axis=0, tiled=True),
            lax.all_gather(w_up, "shard", axis=0, tiled=True),
            lax.all_gather(b_up, "shard", axis=0, tiled=True),
            lax.all_gather(w_down, "shard", axis=0, tiled=True),
            lax.all_gather(b_down, "shard", axis=0, tiled=True),
            lax.all_gather(out_gain, "shard", axis=0, tiled=True),
            lax.all_gather(out_bias, "shard", axis=0, tiled=True),
        )
        layer, tokens_back, local = micro_step(
            tokens[micro], cotangent[micro], seq_lengths[micro, 0], full, index, count
        )
        layers.append(layer)
        inputs_back.append(tokens_back)
        shares = (
            lax.psum_scatter(
                local[0].astype(jnp.bfloat16), "shard", scatter_dimension=0, tiled=True
            ).astype(jnp.float32),
            lax.psum_scatter(
                local[1].astype(jnp.bfloat16), "shard", scatter_dimension=0, tiled=True
            ).astype(jnp.float32),
            lax.psum_scatter(
                local[2].astype(jnp.bfloat16), "shard", scatter_dimension=0, tiled=True
            ).astype(jnp.float32),
            lax.psum_scatter(
                local[3].astype(jnp.bfloat16), "shard", scatter_dimension=0, tiled=True
            ).astype(jnp.float32),
            lax.psum_scatter(
                local[4].astype(jnp.bfloat16), "shard", scatter_dimension=0, tiled=True
            ).astype(jnp.float32),
            lax.psum_scatter(
                local[5].astype(jnp.bfloat16), "shard", scatter_dimension=0, tiled=True
            ).astype(jnp.float32),
            lax.psum_scatter(
                local[6].astype(jnp.bfloat16), "shard", scatter_dimension=0, tiled=True
            ).astype(jnp.float32),
            lax.psum_scatter(
                local[7].astype(jnp.bfloat16), "shard", scatter_dimension=0, tiled=True
            ).astype(jnp.float32),
            lax.psum_scatter(
                local[8].astype(jnp.bfloat16), "shard", scatter_dimension=0, tiled=True
            ).astype(jnp.float32),
            lax.psum_scatter(
                local[9].astype(jnp.bfloat16), "shard", scatter_dimension=0, tiled=True
            ).astype(jnp.float32),
            lax.psum_scatter(
                local[10].astype(jnp.bfloat16), "shard", scatter_dimension=0, tiled=True
            ).astype(jnp.float32),
            lax.psum_scatter(
                local[11].astype(jnp.bfloat16), "shard", scatter_dimension=0, tiled=True
            ).astype(jnp.float32),
            lax.psum_scatter(
                local[12].astype(jnp.bfloat16), "shard", scatter_dimension=0, tiled=True
            ).astype(jnp.float32),
            lax.psum_scatter(
                local[13].astype(jnp.bfloat16), "shard", scatter_dimension=0, tiled=True
            ).astype(jnp.float32),
            lax.psum_scatter(
                local[14].astype(jnp.bfloat16), "shard", scatter_dimension=0, tiled=True
            ).astype(jnp.float32),
        )
        summed = (
            lax.psum(shares[0].astype(jnp.bfloat16), "rep").astype(jnp.float32),
            lax.psum(shares[1].astype(jnp.bfloat16), "rep").astype(jnp.float32),
            lax.psum(shares[2].astype(jnp.bfloat16), "rep").astype(jnp.float32),
            lax.psum(shares[3].astype(jnp.bfloat16), "rep").astype(jnp.float32),
            lax.psum(shares[4].astype(jnp.bfloat16), "rep").astype(jnp.float32),
            lax.psum(shares[5].astype(jnp.bfloat16), "rep").astype(jnp.float32),
            lax.psum(shares[6].astype(jnp.bfloat16), "rep").astype(jnp.float32),
            lax.psum(shares[7].astype(jnp.bfloat16), "rep").astype(jnp.float32),
            lax.psum(shares[8].astype(jnp.bfloat16), "rep").astype(jnp.float32),
            lax.psum(shares[9].astype(jnp.bfloat16), "rep").astype(jnp.float32),
            lax.psum(shares[10].astype(jnp.bfloat16), "rep").astype(jnp.float32),
            lax.psum(shares[11].astype(jnp.bfloat16), "rep").astype(jnp.float32),
            lax.psum(shares[12].astype(jnp.bfloat16), "rep").astype(jnp.float32),
            lax.psum(shares[13].astype(jnp.bfloat16), "rep").astype(jnp.float32),
            lax.psum(shares[14].astype(jnp.bfloat16), "rep").astype(jnp.float32),
        )
        totals = summed if totals is None else jax.tree.map(lambda a, b: a + b, totals, summed)
    return (jnp.stack(layers), jnp.stack(inputs_back)) + tuple(totals)


def solution(mesh):
    return jax.shard_map(
        body,
        mesh=mesh,
        in_specs=(
            P(None, ("rep", "shard"), None),
            P(None, ("rep", "shard"), None),
            P(None, "rep", None),
            P("shard", None),
            P("shard"),
            P("shard", None),
            P("shard", None),
            P("shard"),
            P("shard", None),
            P("shard"),
            P("shard"),
            P("shard"),
            P("shard", None),
            P("shard"),
            P("shard", None),
            P("shard"),
            P("shard"),
            P("shard"),
        ),
        out_specs=(
            P(None, ("rep", "shard"), None),
            P(None, ("rep", "shard"), None),
            P("shard", None),
            P("shard"),
            P("shard", None),
            P("shard", None),
            P("shard"),
            P("shard", None),
            P("shard"),
            P("shard"),
            P("shard"),
            P("shard", None),
            P("shard"),
            P("shard", None),
            P("shard"),
            P("shard"),
            P("shard"),
        ),
        check_vma=False,
    )
```

profile of v0, /device:TPU:1, one launch (start us, length us, event | category | flops | bytes accessed | tf_op | source)
XLA Modules:
  0.0 1368.9 jit_solution(10067084273241734588)
XLA Ops:
  13.3 21.2 %all-gather.26.cloned.1.call-done = bf16[768,768]{1,0:T(8,128)(2,1)} async-done(((bf16[384,768]{1,0:T(8,128)(2,1)}), bf16[768,768]{1,0:T(8,128)(2,1)}) %all-gather.26.cloned.1.call-update) | async-done | bytes 1179664 | tf_op jit(solution)/shard_map/all_gather | solution.py:231
  37.3 21.6 %all-gather.22.cloned.1.call-done = bf16[768,768]{1,0:T(8,128)(2,1)} async-done(((bf16[384,768]{1,0:T(8,128)(2,1)}), bf16[768,768]{1,0:T(8,128)(2,1)}) %all-gather.22.cloned.1.call-update) | async-done | bytes 1179664 | tf_op jit(solution)/shard_map/all_gather | solution.py:230
  115.2 17.8 %all-gather.36.cloned.1.call-done = bf16[768,768]{1,0:T(8,128)(2,1)} async-done(((bf16[384,768]{1,0:T(8,128)(2,1)}), bf16[768,768]{1,0:T(8,128)(2,1)}) %all-gather.36.cloned.1.call-update) | async-done | bytes 1179664 | tf_op jit(solution)/shard_map/all_gather | solution.py:98
  137.3 60.4 %while.57 = (s32[]{:T(128)}, bf16[12,384,64]{1,2,0:T(8,128)(2,1)}, f32[12,384]{1,0:T(8,128)}, bf16[12,384,64]{2,1,0:T(8,128)(2,1)}, bf16[12,768,64]{2,1,0:T(8,12...) while((s32[]{:T(128)}, bf16[12,384,64]{1,2,0:T(8,128)(2,1)}, ...), condition=%wide.region_11.12_spmd.clone, body=%wide.region_8.11_spmd.clone.sunk | while | flops 78151296 | bytes 4155497 | solution.py:115
  211.4 60.5 %while.56 = (s32[]{:T(128)}, bf16[12,384,64]{1,2,0:T(8,128)(2,1)}, f32[12,384]{1,0:T(8,128)}, bf16[12,384,64]{2,1,0:T(8,128)(2,1)}, bf16[12,768,64]{2,1,0:T(8,12...) while((s32[]{:T(128)}, bf16[12,384,64]{1,2,0:T(8,128)(2,1)}, ...), condition=%wide.region_3.4_spmd.clone, body=%wide.region_0.3_spmd.clone.sunk | while | flops 78151296 | bytes 4155497 | solution.py:115
  276.9 4.7 fusion.215
  283.8 24.4 %fusion.96 = (bf16[384,3072]{1,0:T(8,128)(2,1)}, bf16[384,3072]{1,0:T(8,128)(2,1)}, f32[384,3072]{1,0:T(8,128)}) fusion(f32[3072]{0:T(1024)S(1)} %bitcast.360, f32[384,3072]{1,0:T(8,128)S(1)} %fusion.215, bf16[768,3072]{1,0:T(8,128)(2,1)S(1)} %copy-done.77, f32[384,768]{1,0:T(8,128)S(1)} %copy-done.9, f32[768]{0:T(1024)S(1)} %copy-done.60, ...), kind=kOutput, calls=%fused_computation.124 | convolution fusion | flops 1969127424 | bytes 20075520 | tf_op jit(solution)/shard_map/dot_general | solution.py:122
  308.2 27.2 %all-gather.34.cloned.1.call-done = bf16[3072,768]{1,0:T(8,128)(2,1)} async-done(((bf16[1536,768]{1,0:T(8,128)(2,1)}), bf16[3072,768]{1,0:T(8,128)(2,1)}) %all-gather.34.cloned.1.call-update) | async-done | bytes 4718608 | tf_op jit(solution)/shard_map/all_gather | solution.py:239
  335.4 5.3 fusion.228
  349.6 4.5 fusion.229
  369.4 102.6 %while.58 = (s32[]{:T(128)}, bf16[12,384,64]{1,2,0:T(8,128)(2,1)S(1)}, bf16[12,768,64]{1,2,0:T(8,128)(2,1)}, bf16[12,768,64]{1,2,0:T(8,128)(2,1)}, bf16[12,384,6...) while((s32[]{:T(128)}, ...), condition=%wide.region_22.23_spmd.clone, body=%wide.region_20.22_spmd.clone.sunk | while | flops 191766144 | bytes 10242681 | solution.py:160
  475.1 4.3 copy.96
  484.8 102.8 %while.59 = (s32[]{:T(128)}, bf16[12,384,64]{1,2,0:T(8,128)(2,1)S(1)}, bf16[12,768,64]{1,2,0:T(8,128)(2,1)}, bf16[12,768,64]{1,2,0:T(8,128)(2,1)}, bf16[12,384,6...) while((s32[]{:T(128)}, ...), condition=%wide.region_30.31_spmd.clone, body=%wide.region_28.30_spmd.clone.sunk | while | flops 191766144 | bytes 10241657 | solution.py:160
  616.8 13.2 reduce-scatter.45.cloned.1.call-done
  647.7 7.1 convolution_convert_fusion.3
  655.4 7.0 convolution_convert_fusion.2
  662.5 7.2 convolution_convert_fusion.1
  669.8 6.8 convolution_convert_fusion
  681.3 21.7 %reduce-scatter.51.cloned.1.call-done = bf16[384,768]{1,0:T(8,128)(2,1)} async-done(((bf16[768,768]{1,0:T(8,128)(2,1)}), bf16[384,768]{1,0:T(8,128)(2,1)}) %reduce-scatter.51.cloned.1.call-update) | async-done | bytes 589840
  705.1 21.9 %reduce-scatter.55.cloned.1.call-done = bf16[384,768]{1,0:T(8,128)(2,1)} async-done(((bf16[768,768]{1,0:T(8,128)(2,1)}), bf16[384,768]{1,0:T(8,128)(2,1)}) %reduce-scatter.55.cloned.1.call-update) | async-done | bytes 589840
  729.1 22.3 %reduce-scatter.53.cloned.1.call-done = bf16[384,768]{1,0:T(8,128)(2,1)} async-done(((bf16[768,768]{1,0:T(8,128)(2,1)}), bf16[384,768]{1,0:T(8,128)(2,1)}) %reduce-scatter.53.cloned.1.call-update) | async-done | bytes 589840
  753.5 21.9 %reduce-scatter.57.cloned.1.call-done = bf16[384,768]{1,0:T(8,128)(2,1)} async-done(((bf16[768,768]{1,0:T(8,128)(2,1)}), bf16[384,768]{1,0:T(8,128)(2,1)}) %reduce-scatter.57.cloned.1.call-update) | async-done | bytes 589840
  777.6 21.9 %reduce-scatter.31.cloned.1.call-done = bf16[384,768]{1,0:T(8,128)(2,1)} async-done(((bf16[768,768]{1,0:T(8,128)(2,1)}), bf16[384,768]{1,0:T(8,128)(2,1)}) %reduce-scatter.31.cloned.1.call-update) | async-done | bytes 589840 | tf_op jit(solution)/shard_map/reduce_scatter | solution.py:265
  799.4 24.6 %reduce-scatter.33.cloned.1.call-done = bf16[384,768]{1,0:T(8,128)(2,1)} async-done(((bf16[768,768]{1,0:T(8,128)(2,1)}), bf16[384,768]{1,0:T(8,128)(2,1)}) %reduce-scatter.33.cloned.1.call-update) | async-done | bytes 589840 | tf_op jit(solution)/shard_map/reduce_scatter | solution.py:265
  824.0 62.9 %reduce-scatter.35.cloned.1.call-done = bf16[384,3072]{1,0:T(8,128)(2,1)} async-done(((bf16[768,3072]{1,0:T(8,128)(2,1)}), bf16[384,3072]{1,0:T(8,128)(2,1)}) %reduce-scatter.35.cloned.1.call-update) | async-done | bytes 2359312 | tf_op jit(solution)/shard_map/reduce_scatter | solution.py:277
  886.9 63.0 %reduce-scatter.37.cloned.1.call-done = bf16[384,3072]{1,0:T(8,128)(2,1)} async-done(((bf16[768,3072]{1,0:T(8,128)(2,1)}), bf16[384,3072]{1,0:T(8,128)(2,1)}) %reduce-scatter.37.cloned.1.call-update) | async-done | bytes 2359312 | tf_op jit(solution)/shard_map/reduce_scatter | solution.py:277
  949.9 62.3 %reduce-scatter.39.cloned.1.call-done = bf16[1536,768]{1,0:T(8,128)(2,1)} async-done(((bf16[3072,768]{1,0:T(8,128)(2,1)}), bf16[1536,768]{1,0:T(8,128)(2,1)}) %reduce-scatter.39.cloned.1.call-update) | async-done | bytes 2359312 | tf_op jit(solution)/shard_map/reduce_scatter | solution.py:283
  1012.2 62.3 %reduce-scatter.41.cloned.1.call-done = bf16[1536,768]{1,0:T(8,128)(2,1)} async-done(((bf16[3072,768]{1,0:T(8,128)(2,1)}), bf16[1536,768]{1,0:T(8,128)(2,1)}) %reduce-scatter.41.cloned.1.call-update) | async-done | bytes 2359312 | tf_op jit(solution)/shard_map/reduce_scatter | solution.py:283
  1083.9 5.9 all-reduce.20
  1091.2 60.6 %all-reduce.18 = (bf16[384]{0:T(512)(128)(2,1)S(1)}, bf16[384]{0:T(512)(128)(2,1)S(1)}, bf16[384]{0:T(512)(128)(2,1)S(1)}, bf16[384]{0:T(512)(128)(2,1)S(1)}, bf...) all-reduce(bf16[384]{0:T(512)(128)(2,1)S(1)} %dynamic-slice.5, ...), channel_id=1, replica_groups=mesh['rep'=16,'shard'=2] {'rep'}, use_global_device_ids=true, to_apply=%region_41.42 | all-reduce | flops 9216 | bytes 36864 | tf_op jit(solution)/shard_map/psum | solution.py:298
  1163.1 183.8 %all-reduce.23.cloned.1.call-done = (bf16[384,768]{0,1:T(8,128)(2,1)}, bf16[384,768]{0,1:T(8,128)(2,1)}, bf16[384,768]{0,1:T(8,128)(2,1)}, bf16[384,768]{0,1:T(8...) async-done(((bf16[384,768]{0,1:T(8,128)(2,1)}, ...) | async-done | bytes 14155792 | tf_op jit(solution)/shard_map/psum | solution.py:297
  1353.4 4.5 convert_add_fusion
  (733 shorter events, 539.1 us)
Async XLA Ops:
  7.2 27.3 %copy-start.78 = (bf16[2,384,768]{2,1,0:T(8,128)(2,1)S(1)}, bf16[2,384,768]{2,1,0:T(8,128)(2,1)}, u32[]{:S(2)}) copy-start(bf16[2,384,768]{2,1,0:T(8,128)(2,1)} %param.26) | copy-start | bytes 3538948
  7.2 27.3 %all-gather.26.cloned.1.call-start = ((), (), s32[]{:S(2)}) async-start(), calls=%async_computation.17 | async-start | bytes 1769472 | tf_op jit(solution)/shard_map/all_gather | solution.py:231
  7.9 50.9 %all-gather.22.cloned.1.call-start = ((), (), s32[]{:S(2)}) async-start(), calls=%async_computation.15 | async-start | bytes 1769472 | tf_op jit(solution)/shard_map/all_gather | solution.py:230
  8.7 96.5 %all-gather.20.cloned.1.call-start = ((), (), s32[]{:S(2)}) async-start(), calls=%async_computation.14 | async-start | bytes 1769472 | tf_op jit(solution)/shard_map/all_gather | solution.py:228
  9.4 101.8 %all-gather.38.cloned.1.call-start = ((), (), s32[]{:S(2)}) async-start(), calls=%async_computation.23 | async-start | bytes 1769472 | tf_op jit(solution)/shard_map/all_gather | solution.py:99
  37.2 95.8 %all-gather.36.cloned.1.call-start = ((), (), s32[]{:S(2)}) async-start(), calls=%async_computation.22 | async-start | bytes 1769472 | tf_op jit(solution)/shard_map/all_gather | solution.py:98
  61.6 136.2 %all-gather.30.cloned.1.call-start = ((), (), s32[]{:S(2)}) async-start(), calls=%async_computation.19 | async-start | bytes 1769472 | tf_op jit(solution)/shard_map/all_gather | solution.py:233
  62.2 140.7 %all-gather.28.cloned.1.call-start = ((), (), s32[]{:S(2)}) async-start(), calls=%async_computation.18 | async-start | bytes 1769472 | tf_op jit(solution)/shard_map/all_gather | solution.py:99
  64.3 142.8 %all-gather.24.cloned.1.call-start = ((), (), s32[]{:S(2)}) async-start(), calls=%async_computation.16 | async-start | bytes 1769472 | tf_op jit(solution)/shard_map/all_gather | solution.py:98
  65.8 210.6 %all-gather.32.cloned.1.call-start = ((), (), s32[]{:S(2)}) async-start(), calls=%async_computation.20 | async-start | bytes 7077888 | tf_op jit(solution)/shard_map/all_gather | solution.py:237
  66.7 30.1 %copy-start.75 = (bf16[384]{0:T(512)(128)(2,1)S(1)}, bf16[384]{0:T(512)(128)(2,1)}, u32[]{:S(2)}) copy-start(bf16[384]{0:T(512)(128)(2,1)} %param.42) | copy-start | bytes 2308
  66.7 34.2 %copy-start.76 = (bf16[384]{0:T(512)(128)(2,1)S(1)}, bf16[384]{0:T(512)(128)(2,1)}, u32[]{:S(2)}) copy-start(bf16[384]{0:T(512)(128)(2,1)} %param.43) | copy-start | bytes 2308
  66.7 268.7 %all-gather.34.cloned.1.call-start = ((), (), s32[]{:S(2)}) async-start(), calls=%async_computation.21 | async-start | bytes 7077888 | tf_op jit(solution)/shard_map/all_gather | solution.py:239
  67.3 538.5 %reduce-scatter.43.cloned.1.call-start = ((), (), s32[]{:S(2)}) async-start(), calls=%async_computation.30 | async-start | bytes 3538944
  275.2 65.8 %copy-start.36 = (f32[384]{0:T(512)}, f32[384]{0:T(512)S(1)}, u32[]{:S(2)}) copy-start(f32[384]{0:T(512)S(1)} %broadcast_multiply_fusion.11) | copy-start | bytes 4612
  276.4 64.6 %copy-start.55 = (f32[384]{0:T(512)}, f32[384]{0:T(512)S(1)}, u32[]{:S(2)}) copy-start(f32[384]{0:T(512)S(1)} %add_rsqrt_fusion.3) | copy-start | bytes 4612
  283.8 51.6 %copy-start.62 = (f32[768]{0:T(1024)S(1)}, f32[768]{0:T(1024)}, u32[]{:S(2)}) copy-start(f32[768]{0:T(1024)} %reshape.331) | copy-start | bytes 9220
  479.4 150.6 %reduce-scatter.45.cloned.1.call-start = ((), (), s32[]{:S(2)}) async-start(), calls=%async_computation.31 | async-start | bytes 3538944
  595.1 81.6 %reduce-scatter.47.cloned.1.call-start = ((), (), s32[]{:S(2)}) async-start(), calls=%async_computation.32 | async-start | bytes 1769472
  600.4 78.8 %reduce-scatter.49.cloned.1.call-start = ((), (), s32[]{:S(2)}) async-start(), calls=%async_computation.33 | async-start | bytes 1769472
  605.7 97.3 %reduce-scatter.51.cloned.1.call-start = ((), (), s32[]{:S(2)}) async-start(), calls=%async_computation.34 | async-start | bytes 1769472
  611.2 115.8 %reduce-scatter.55.cloned.1.call-start = ((), (), s32[]{:S(2)}) async-start(), calls=%async_computation.36 | async-start | bytes 1769472
  616.8 134.7 %reduce-scatter.53.cloned.1.call-start = ((), (), s32[]{:S(2)}) async-start(), calls=%async_computation.35 | async-start | bytes 1769472
  635.5 140.0 %reduce-scatter.57.cloned.1.call-start = ((), (), s32[]{:S(2)}) async-start(), calls=%async_computation.37 | async-start | bytes 1769472
  641.1 158.3 %reduce-scatter.31.cloned.1.call-start = ((), (), s32[]{:S(2)}) async-start(), calls=%async_computation.24 | async-start | bytes 1769472 | tf_op jit(solution)/shard_map/reduce_scatter | solution.py:265
  644.1 179.9 %reduce-scatter.33.cloned.1.call-start = ((), (), s32[]{:S(2)}) async-start(), calls=%async_computation.25 | async-start | bytes 1769472 | tf_op jit(solution)/shard_map/reduce_scatter | solution.py:265
  647.0 239.9 %reduce-scatter.35.cloned.1.call-start = ((), (), s32[]{:S(2)}) async-start(), calls=%async_computation.26 | async-start | bytes 7077888 | tf_op jit(solution)/shard_map/reduce_scatter | solution.py:277
  654.8 295.1 %reduce-scatter.37.cloned.1.call-start = ((), (), s32[]{:S(2)}) async-start(), calls=%async_computation.27 | async-start | bytes 7077888 | tf_op jit(solution)/shard_map/reduce_scatter | solution.py:277
  662.5 349.8 %reduce-scatter.39.cloned.1.call-start = ((), (), s32[]{:S(2)}) async-start(), calls=%async_computation.28 | async-start | bytes 7077888 | tf_op jit(solution)/shard_map/reduce_scatter | solution.py:283
  669.7 404.8 %reduce-scatter.41.cloned.1.call-start = ((), (), s32[]{:S(2)}) async-start(), calls=%async_computation.29 | async-start | bytes 7077888 | tf_op jit(solution)/shard_map/reduce_scatter | solution.py:283
  676.6 670.3 %all-reduce.23.cloned.1.call-start = ((), (), s32[]{:S(2)}) async-start(), calls=%async_computation.38 | async-start | bytes 28311552 | tf_op jit(solution)/shard_map/psum | solution.py:297
  1083.2 68.6 %copy-start.11 = (bf16[768,768]{1,0:T(8,128)(2,1)S(1)}, bf16[768,768]{1,0:T(8,128)(2,1)}, u32[]{:S(2)}) copy-start(bf16[768,768]{1,0:T(8,128)(2,1)} %all-gather.22.cloned.1.call-done) | copy-start | bytes 3538948
  (85 other events, 310.8 us)
Sparse Core Ops, SparseCore 0:
  9.6 24.8 all-gather.25
  36.0 22.7 all-gather.21
  60.4 22.8 all-gather.19
  85.2 22.9 all-gather.37
  110.2 22.7 all-gather.35
  134.4 22.7 all-gather.29
  159.3 22.7 all-gather.27
  184.2 22.7 all-gather.23
  208.6 62.6 all-gather.31
  272.7 62.6 all-gather.33
  479.6 34.7 reduce-scatter.42
  595.2 34.7 reduce-scatter.44
  632.8 21.7 reduce-scatter.46
  657.4 21.7 reduce-scatter.48
  681.2 21.7 reduce-scatter.50
  705.2 21.7 reduce-scatter.54
  729.7 21.7 reduce-scatter.52
  753.6 21.7 reduce-scatter.56
  777.7 21.7 reduce-scatter.30
  802.2 21.7 reduce-scatter.32
  826.9 59.9 reduce-scatter.34
  889.9 59.9 reduce-scatter.36
  952.2 59.9 reduce-scatter.38
  1014.5 59.9 reduce-scatter.40
  1081.5 265.3 all-reduce.22
where the time goes:
time: 1380 us; the launch traced here: 1370 us
  waiting for transfers between devices  674 us (49%)
  matrix products  392 us (28%)
  local copies, waits for them, and re-layouts  133 us (10%)
  blocking collectives  97.4 us (7%)
  other arithmetic  53.2 us (4%)
  between operations  16.8 us (1%)
    psum x1, waiting for transfers between devices, body(): lax.psum(shares[0].astype(jnp.bfloat16), 'rep').astype(jnp.float32)  184 us
    dot_general x60, matrix products, outer_rows(): lax.dot_general(left, right, (((0,), (0,)), ((), ())), preferred_element_...  135 us
    reduce_scatter x2, waiting for transfers between devices, body(): lax.psum_scatter(local[9].astype(jnp.bfloat16), 'shard', scatter_dimensio...  126 us
    reduce_scatter x2, waiting for transfers between devices, body(): lax.psum_scatter(local[11].astype(jnp.bfloat16), 'shard', scatter_dimensi...  125 us
    dot_general x84, matrix products, back_rows(): lax.dot_general(left, right, (((1,), (1,)), ((), ())), preferred_element_...  124 us
    unnamed x33, waiting for transfers between devices  105 us
    unnamed x235, local copies, waits for them, and re-layouts  62.7 us
    psum x1, blocking collectives, body(): lax.psum(shares[1].astype(jnp.bfloat16), 'rep').astype(jnp.float32)  60.6 us
  transfers between devices with their start and end apart: 25, of which 18 were waited for; matrix products, arithmetic and copies ran while one was open for 30% of the time, Pallas kernels for 0%

commit v1 on v0

v1 whole, which is shorter than its diff:
```python
import functools

import jax
import jax.numpy as jnp
from jax import lax
from jax.experimental import pallas as pl
from jax.experimental.pallas import tpu as pltpu
from jax.sharding import PartitionSpec as P

D = 768
H = 12
DH = 64
PAIR = 2 * DH
EPS = 1e-12
BIG = 1e30
SCALE = DH ** (-0.5)
ROWS = 256
f32 = jnp.float32
bf16 = jnp.bfloat16


def mm(left, right):
    return jnp.dot(left, right, preferred_element_type=f32)


def mm_nt(left, right):
    return lax.dot_general(left, right, (((1,), (1,)), ((), ())), preferred_element_type=f32)


def mm_tn(left, right):
    return lax.dot_general(left, right, (((0,), (0,)), ((), ())), preferred_element_type=f32)


def segment_ids(row, count):
    bounds = jnp.cumsum(row[:-1])
    places = jnp.arange(count, dtype=jnp.int32)
    return jnp.sum((places[:, None] >= bounds[None, :]).astype(jnp.int32), axis=1)


def mask_columns(ids):
    first = (ids == 0).astype(f32)[:, None]
    other = 1.0 - first
    lane = lax.broadcasted_iota(jnp.int32, (1, PAIR), 1) % DH
    on_query = jnp.where(lane == 0, -BIG * first, jnp.where(lane == 1, -BIG * other, 0.0))
    on_key = jnp.where(lane == 0, other, jnp.where(lane == 1, first, 0.0))
    return on_query.astype(bf16), on_key.astype(bf16)


def forward_heads(q_ref, k_ref, v_ref, mq_ref, mk_ref, attn_ref, lse_ref):
    lane = lax.broadcasted_iota(jnp.int32, (1, PAIR), 1)
    low = lane < DH
    keys, values, mk = k_ref[...], v_ref[...], mk_ref[...]
    one = jnp.ones_like(values)
    sides = []
    for own in (low, jnp.logical_not(low)):
        sides.append((own, jnp.where(own, keys, mk), jnp.where(own, values, one)))
    count = q_ref.shape[0]
    block = min(ROWS, count)
    for start in range(0, count, block):
        rows = pl.ds(start, block)
        query, mq = q_ref[rows, :] * SCALE, mq_ref[rows, :]
        outs = []
        for own, some_keys, some_values in sides:
            scores = mm_nt(jnp.where(own, query, mq), some_keys)
            top = jnp.max(scores, axis=1, keepdims=True)
            expo = jnp.exp(scores - top).astype(bf16)
            mixed = mm(expo, some_values)
            total = pltpu.roll(mixed, DH, 1)
            outs.append((mixed / total, top + jnp.log(total)))
        attn_ref[rows, :] = jnp.where(low, outs[0][0], outs[1][0]).astype(bf16)
        lse_ref[rows, :] = jnp.where(low, outs[0][1], outs[1][1])


def three_parts(value):
    first = value.astype(bf16).astype(f32)
    rest = value - first
    second = rest.astype(bf16).astype(f32)
    return first, second, rest - second


def backward_heads(
    q_ref, k_ref, v_ref, mq_ref, mk_ref, attn_ref, lse_ref, grad_ref, dq_ref, dk_ref, dv_ref
):
    lane = lax.broadcasted_iota(jnp.int32, (1, PAIR), 1)
    place = lane % DH
    low = lane < DH
    query, mq, grad = q_ref[...] * SCALE, mq_ref[...], grad_ref[...]
    product = grad.astype(f32) * attn_ref[...].astype(f32)
    lse = three_parts(-pltpu.roll(lse_ref[...], DH, 1))
    count_keys = k_ref.shape[0]
    block = min(ROWS, count_keys)
    sides = []
    for own in (low, jnp.logical_not(low)):
        delta = three_parts(-jnp.sum(jnp.where(own, product, 0.0), axis=1, keepdims=True))
        more = jnp.where(place == 2, lse[0], jnp.where(place == 3, lse[1], lse[2]))
        more = jnp.where(place < 2, mq, jnp.where(place < 5, more, 0.0).astype(bf16))
        some_query = jnp.where(own, query, more)
        more = jnp.where(place == 0, delta[0], jnp.where(place == 1, delta[1], delta[2]))
        some_grad = jnp.where(own, grad, jnp.where(place < 3, more, 0.0).astype(bf16))
        sides.append((own, some_query, some_grad, None))
    totals = [None, None]
    for start in range(0, count_keys, block):
        rows = pl.ds(start, block)
        keys, values, mk = k_ref[rows, :], v_ref[rows, :], mk_ref[rows, :]
        ones = jnp.ones_like(values)
        zeros = jnp.zeros_like(values)
        more_keys = jnp.where(place < 2, mk, jnp.where(place < 5, ones, zeros))
        more_values = jnp.where(place < 3, ones, zeros)
        parts = []
        for side in range(2):
            own, some_query, some_grad, _ = sides[side]
            some_keys = jnp.where(own, keys, more_keys)
            some_values = jnp.where(own, values, more_values)
            probs = jnp.exp(mm_nt(some_keys, some_query))
            slope = (probs * mm_nt(some_values, some_grad)).astype(bf16)
            dv = mm(probs.astype(bf16), some_grad)
            dk = mm(slope, some_query)
            dq = mm_tn(slope, some_keys)
            totals[side] = dq if totals[side] is None else totals[side] + dq
            parts.append((dk, dv))
        dk_ref[rows, :] = jnp.where(low, parts[0][0], parts[1][0]).astype(bf16)
        dv_ref[rows, :] = jnp.where(low, parts[0][1], parts[1][1]).astype(bf16)
    dq_ref[...] = (jnp.where(low, totals[0], totals[1]) * SCALE).astype(bf16)


def head_block(rows, offset):
    return pl.BlockSpec((rows, PAIR), lambda i: (0, i + offset))


def fixed_block(rows):
    return pl.BlockSpec((rows, PAIR), lambda i: (0, 0))


def attention_forward(query_array, key_array, offsets, mq, mk):
    count, keys = query_array.shape[0], key_array.shape[0]
    pairs = H * DH // PAIR
    return pl.pallas_call(
        forward_heads,
        grid=(pairs,),
        out_shape=(
            jax.ShapeDtypeStruct((count, D), bf16),
            jax.ShapeDtypeStruct((count, D), f32),
        ),
        in_specs=[
            head_block(count, 0),
            head_block(keys, offsets[0]),
            head_block(keys, offsets[1]),
            fixed_block(count),
            fixed_block(keys),
        ],
        out_specs=(head_block(count, 0), head_block(count, 0)),
        cost_estimate=pl.CostEstimate(
            flops=16 * count * keys * D, bytes_accessed=8 * (count + keys) * D, transcendentals=count * keys * H
        ),
        name="attention_forward",
    )(query_array, key_array, key_array, mq, mk)


def attention_backward(query_array, key_array, offsets, mq, mk, attn, lse, grad):
    count, keys = query_array.shape[0], key_array.shape[0]
    pairs = H * DH // PAIR
    return pl.pallas_call(
        backward_heads,
        grid=(pairs,),
        out_shape=(
            jax.ShapeDtypeStruct((count, D), bf16),
            jax.ShapeDtypeStruct((keys, D), bf16),
            jax.ShapeDtypeStruct((keys, D), bf16),
        ),
        in_specs=[
            head_block(count, 0),
            head_block(keys, offsets[0]),
            head_block(keys, offsets[1]),
            fixed_block(count),
            fixed_block(keys),
            head_block(count, 0),
            head_block(count, 0),
            head_block(count, 0),
        ],
        out_specs=(head_block(count, 0), head_block(keys, 0), head_block(keys, 0)),
        cost_estimate=pl.CostEstimate(
            flops=40 * count * keys * D, bytes_accessed=16 * (count + keys) * D, transcendentals=count * keys * H
        ),
        name="attention_backward",
    )(query_array, key_array, key_array, mq, mk, attn, lse, grad)


def normalize(rows):
    mean = jnp.mean(rows, axis=-1, keepdims=True)
    centered = rows - mean
    inverse = lax.rsqrt(jnp.mean(centered * centered, axis=-1, keepdims=True) + EPS)
    return centered * inverse, inverse


def norm_back(grad, normed, inverse, gain):
    scaled = grad * gain
    first = jnp.mean(scaled, axis=-1, keepdims=True)
    second = jnp.mean(scaled * normed, axis=-1, keepdims=True)
    return inverse * (scaled - first - normed * second)


def swap(value, axis, size, move):
    return lax.ppermute(value, axis, [(i, move(i)) for i in range(size)])


def put(buffer, value, index, axis=0):
    return lax.dynamic_update_slice_in_dim(buffer, value, index * value.shape[axis], axis)


def pick(value, index, parts, axis=0):
    size = value.shape[axis] // parts
    return lax.dynamic_slice_in_dim(value, index * size, size, axis)


class Places:
    def __init__(self):
        self.reps = lax.axis_size("rep")
        self.shards = lax.axis_size("shard")
        self.rep = lax.axis_index("rep")
        self.shard = lax.axis_index("shard")
        self.core = self.rep % 2


def gather_rows(at, own):
    half = own.shape[0] // 2
    out = jnp.zeros((at.shards * own.shape[0],) + own.shape[1:], own.dtype)
    out = put(out, own, at.shard)
    mine = pick(own, at.core, 2)
    for step in range(1, at.shards):
        there = swap(mine, "shard", at.shards, lambda i: (i + at.shards - step) % at.shards)
        other = swap(there, "rep", at.reps, lambda i: i ^ 1)
        block = (at.shard + step) % at.shards * 2
        out = put(out, there, block + at.core)
        out = put(out, other, block + 1 - at.core)
    return out


def reduce_rows(at, grad):
    shards, columns = at.shards, grad.shape[1]
    rows = grad.shape[0] // shards
    value = grad.reshape(shards * 2, rows // 2, columns)
    value = grad.reshape(shards, 2, rows // 2, columns)
    mine = lax.dynamic_index_in_dim(value, at.core, 1, False)
    away = lax.dynamic_index_in_dim(value, 1 - at.core, 1, False).astype(bf16)
    value = mine.astype(f32) + swap(away, "rep", at.reps, lambda i: i ^ 1).astype(f32)
    total = lax.dynamic_index_in_dim(value, at.shard, 0, False)
    for step in range(1, shards):
        away = lax.dynamic_index_in_dim(value, (at.shard + step) % shards, 0, False).astype(bf16)
        total = total + swap(away, "shard", shards, lambda i: (i + step) % shards).astype(f32)
    stages = []
    bit = 2
    while bit < at.reps:
        axis = 0 if total.shape[0] % 32 == 0 else 1
        stages.append((bit, axis))
        up = (at.rep // bit) % 2
        mine, away = pick(total, up, 2, axis), pick(total, 1 - up, 2, axis).astype(bf16)
        move = functools.partial(lambda b, i: i ^ b, bit)
        total = mine + swap(away, "rep", at.reps, move).astype(f32)
        bit *= 2
    total = total.astype(bf16)
    for bit, axis in reversed(stages):
        up = (at.rep // bit) % 2
        move = functools.partial(lambda b, i: i ^ b, bit)
        other = swap(total, "rep", at.reps, move)
        shape = list(total.shape)
        shape[axis] *= 2
        both = jnp.zeros(shape, bf16)
        total = put(put(both, total, up, axis), other, 1 - up, axis)
    other = swap(total, "rep", at.reps, lambda i: i ^ 1)
    first = jnp.where(at.core == 0, total, other)
    second = jnp.where(at.core == 0, other, total)
    return jnp.concatenate([first, second], axis=0).astype(f32)


def spread(at, value):
    micro, shards = value.shape[0], at.shards
    parts = []
    for step in range(micro):
        moves = [(i, (i + step) % micro * (shards // micro) + i // micro) for i in range(shards)]
        part = lax.dynamic_index_in_dim(value, (at.shard + step) % micro, 0, False)
        if any(a != b for a, b in moves):
            part = lax.ppermute(part, "shard", moves)
        parts.append(part)
    return jnp.concatenate(parts, axis=0)


def collect(at, value, micro):
    shards = at.shards
    slots = value.shape[0] // micro
    out = jnp.zeros((micro, slots) + value.shape[1:], value.dtype)
    for step in range(micro):
        moves = [((i + step) % micro * (shards // micro) + i // micro, i) for i in range(shards)]
        part = value[step * slots : (step + 1) * slots]
        if any(a != b for a, b in moves):
            part = lax.ppermute(part, "shard", moves)
        out = lax.dynamic_update_index_in_dim(out, part, (at.shard + step) % micro, 0)
    return out


def body(
    tokens,
    cotangent,
    seq_lengths,
    w_query,
    b_query,
    w_key,
    w_value,
    b_value,
    w_attn,
    b_attn,
    norm_gain,
    norm_bias,
    w_up,
    b_up,
    w_down,
    b_down,
    out_gain,
    out_bias,
):
    at = Places()
    shards = at.shards
    micro, slots = tokens.shape[0], tokens.shape[1]
    span = shards // micro
    count = micro * slots
    x = spread(at, tokens)
    w_three = gather_rows(at, jnp.concatenate([w_query, w_key, w_value], axis=1))
    part = w_query.shape[0]
    wide = b_up.shape[0] // part
    vectors = jnp.concatenate(
        [
            jnp.stack(
                [b_query, b_value, b_attn, norm_gain, norm_bias, b_down, out_gain, out_bias]
            ),
            b_up.reshape(wide, part),
            jnp.zeros((16 - 8 - wide, part), bf16),
        ],
        axis=0,
    )
    table = put(jnp.zeros((shards,) + vectors.shape, bf16), vectors[None], at.shard)
    for step in range(1, shards):
        there = swap(vectors, "shard", shards, lambda i: (i + shards - step) % shards)
        table = put(table, there[None], (at.shard + step) % shards)
    table = table.astype(f32)
    (c_query, c_value, c_attn, c_gain, c_bias, c_down, c_out_gain, c_out_bias) = [
        table[:, i].reshape(1, D) for i in range(8)
    ]
    c_up = table[:, 8 : 8 + wide].reshape(1, D * wide)
    w_proj = gather_rows(at, w_attn)
    full_up = gather_rows(at, w_up)
    full_down = gather_rows(at, w_down)
    slope_in = spread(at, cotangent)

    group = slots * shards
    which, inner = at.shard // span, at.shard % span
    row = lax.dynamic_index_in_dim(seq_lengths[:, 0], which, 0, False)
    ids = segment_ids(row, group)

    def ids_of(device):
        parts = []
        for step in range(micro):
            source = micro * device + (which + micro - step) % micro
            parts.append(lax.dynamic_slice_in_dim(ids, source * slots, slots))
        return jnp.concatenate(parts)

    query_ids = ids_of(inner)
    nseq = seq_lengths.shape[-1] - 1
    valid = (query_ids < nseq).astype(f32)[:, None]
    three = mm(x, w_three) + jnp.concatenate([c_query, jnp.zeros_like(c_query), c_value], axis=1)
    three = three.astype(bf16)
    base = D // PAIR
    offsets = (base, 2 * base)
    key_array = three
    key_ids = [query_ids]
    if span > 1:
        offsets = (0, base)
        own = three[:, D:]
        parts = [own]
        for step in range(1, span):
            moves = [(i, i // span * span + (i + span - step) % span) for i in range(shards)]
            parts.append(lax.ppermute(own, "shard", moves))
            key_ids.append(ids_of((inner + step) % span))
        key_array = jnp.concatenate(parts, axis=0)
    mq, _ = mask_columns(query_ids)
    _, mk = mask_columns(jnp.concatenate(key_ids))
    attn, lse = attention_forward(three, key_array, offsets, mq, mk)

    normed_one, inverse_one = normalize(x.astype(f32) + mm(attn, w_proj) + c_attn)
    hidden = normed_one * c_gain + c_bias
    hidden_low = hidden.astype(bf16)
    pre = mm(hidden_low, full_up) + c_up
    lower = 0.5 * (1.0 + lax.erf(pre * 0.7071067811865476))
    active = (pre * lower).astype(bf16)
    density = jnp.exp(-0.5 * pre * pre) * 0.3989422804014327
    gelu_slope = lower + pre * density
    normed_two, inverse_two = normalize(hidden + mm(active, full_down) + c_down)
    layer = (normed_two * c_out_gain + c_out_bias).astype(bf16)
    grad_out = slope_in.astype(f32) * valid
    d_out_gain = jnp.sum(grad_out * normed_two, axis=0)
    d_out_bias = jnp.sum(grad_out, axis=0)
    grad_second = norm_back(grad_out, normed_two, inverse_two, c_out_gain)
    grad_branch = grad_second.astype(bf16)
    d_down = jnp.sum(grad_branch.astype(f32), axis=0)
    g_down = mm_tn(active, grad_branch)
    grad_pre = (mm_nt(grad_branch, full_down) * gelu_slope).astype(bf16)
    d_up = jnp.sum(grad_pre.astype(f32), axis=0)
    g_up = mm_tn(hidden_low, grad_pre)
    grad_hidden = mm_nt(grad_pre, full_up) + grad_second
    d_gain = jnp.sum(grad_hidden * normed_one, axis=0)
    d_bias = jnp.sum(grad_hidden, axis=0)
    grad_first = norm_back(grad_hidden, normed_one, inverse_one, c_gain)
    grad_proj = grad_first.astype(bf16)
    d_attn = jnp.sum(grad_proj.astype(f32), axis=0)
    g_attn = mm_tn(attn, grad_proj)
    grad_attn = mm_nt(grad_proj, w_proj).astype(bf16)
    dq, dk, dv = attention_backward(three, key_array, offsets, mq, mk, attn, lse, grad_attn)
    if span > 1:
        both = jnp.concatenate([dk, dv], axis=1)
        total = both[:count].astype(f32)
        for step in range(1, span):
            moves = [(i, i // span * span + (i + step) % span) for i in range(shards)]
            away = both[step * count : (step + 1) * count]
            total = total + lax.ppermute(away, "shard", moves).astype(f32)
        dk, dv = total[:, :D].astype(bf16), total[:, D:].astype(bf16)
    d_three = jnp.concatenate([dq, dk, dv], axis=1)
    d_query = jnp.sum(dq.astype(f32), axis=0)
    d_value = jnp.sum(dv.astype(f32), axis=0)
    g_three = mm_tn(x, d_three)
    back = (grad_first + mm_nt(d_three, w_three)).astype(bf16)

    sums = jnp.concatenate(
        [
            jnp.stack([d_query, d_value, d_attn, d_gain, d_bias, d_down, d_out_gain, d_out_bias]).reshape(
                8, shards, part
            ),
            d_up.reshape(shards, wide, part).transpose(1, 0, 2),
            jnp.zeros((PAIR - 8 - wide, shards, part), f32),
        ],
        axis=0,
    )
    sums = sums.reshape(PAIR, D).T
    r_down = reduce_rows(at, g_down)
    r_up = reduce_rows(at, g_up)
    r_attn = reduce_rows(at, g_attn)
    r_three = reduce_rows(at, jnp.concatenate([g_three, sums], axis=1))
    small = r_three[:, 3 * D :].T
    return (
        collect(at, layer, micro),
        collect(at, back, micro),
        r_three[:, :D],
        small[0],
        r_three[:, D : 2 * D],
        r_three[:, 2 * D : 3 * D],
        small[1],
        r_attn,
        small[2],
        small[3],
        small[4],
        r_up,
        small[8 : 8 + wide].reshape(wide * part),
        r_down,
        small[5],
        small[6],
        small[7],
    )


def solution(mesh):
    rows, vector = P("shard", None), P("shard")
    tokens = P(None, ("rep", "shard"), None)
    weights = (rows, vector, rows, rows, vector, rows, vector, vector, vector)
    weights += (rows, vector, rows, vector, vector, vector)
    return jax.shard_map(
        body,
        mesh=mesh,
        in_specs=(tokens, tokens, P(None, "rep", None)) + weights,
        out_specs=(tokens, tokens) + weights,
        check_vma=False,
    )
```

time: 1380 us -> 482 us (0.35)
  waiting for transfers between devices: 674 us -> 142 us
  matrix products: 392 us -> 77.9 us
  blocking collectives: 97.4 us -> 0 us
  starting transfers between devices: 1.23 us -> 63.7 us
  Pallas kernels: 0 us -> 44.8 us
  local copies, waits for them, and re-layouts: 133 us -> 103 us
  between operations: 16.8 us -> 2.67 us
    dot_general x204 -> x12, matrix products: 392 us -> 77.9 us  [the longest x4 27.1 us: mm_nt(): lax.dot_general(left, right, (((1,), (1,)), ((), ())), preferred_element_...]
    reduce_scatter x6 -> x0, waiting for transfers between devices: 297 us -> none  [the longest x2 126 us: body(): lax.psum_scatter(local[9].astype(jnp.bfloat16), 'shard', scatter_dimensio...]
    psum x1 -> x0, waiting for transfers between devices: 184 us -> none  [body(): lax.psum(shares[0].astype(jnp.bfloat16), 'rep').astype(jnp.float32)]
    ppermute x0 -> x49, waiting for transfers between devices: none -> 142 us  [the longest x45 142 us: swap(): return lax.ppermute(value, axis, [(i, move(i)) for i in range(size)])]
    unnamed x33 -> x0, waiting for transfers between devices: 105 us -> none
    all_gather x10 -> x0, waiting for transfers between devices: 88 us -> none  [the longest x1 27.2 us: body(): lax.all_gather(w_down, 'shard', axis=0, tiled=True)]
    ppermute x0 -> x49, starting transfers between devices: none -> 63.7 us  [the longest x45 62.8 us: swap(): return lax.ppermute(value, axis, [(i, move(i)) for i in range(size)])]
    psum x1 -> x0, blocking collectives: 60.6 us -> none  [body(): lax.psum(shares[1].astype(jnp.bfloat16), 'rep').astype(jnp.float32)]
  transfers between devices with their start and end apart: 25 -> 49, of which waited for: 18 -> 19; matrix products, arithmetic and copies ran while one was open for 30% -> 32% of each run, Pallas kernels for 0% -> 4%
where the time goes in v1:
time: 482 us; the launch traced here: 474 us
  waiting for transfers between devices  142 us (29%)
  local copies, waits for them, and re-layouts  103 us (21%)
  matrix products  77.9 us (16%)
  starting transfers between devices  63.7 us (13%)
  Pallas kernels  44.8 us (9%)
  other arithmetic  40.1 us (8%)
    ppermute x45, waiting for transfers between devices, swap(): return lax.ppermute(value, axis, [(i, move(i)) for i in range(size)])  142 us
    ppermute x45, starting transfers between devices, swap(): return lax.ppermute(value, axis, [(i, move(i)) for i in range(size)])  62.8 us
    dot_general x4, matrix products, mm_nt(): lax.dot_general(left, right, (((1,), (1,)), ((), ())), preferred_element_...  27.1 us
    dynamic_update_slice x35, local copies, waits for them, and re-layouts, put(): lax.dynamic_update_slice_in_dim(buffer, value, index * value.shape[axis],...  26.9 us
    pallas_call x1, Pallas kernels, attention_backward(): pl.pallas_call(backward_heads, grid=(pairs,), out_shape=(jax.ShapeDtypeSt...  26.3 us
    dot_general x4, matrix products, mm(): return jnp.dot(left, right, preferred_element_type=f32)  26.1 us
    dot_general x4, matrix products, mm_tn(): lax.dot_general(left, right, (((0,), (0,)), ((), ())), preferred_element_...  24.7 us
    pallas_call x1, Pallas kernels, attention_forward(): pl.pallas_call(forward_heads, grid=(pairs,), out_shape=(jax.ShapeDtypeStr...  18.5 us
  transfers between devices with their start and end apart: 49, of which 19 were waited for; matrix products, arithmetic and copies ran while one was open for 32% of the time, Pallas kernels for 4%

profile of v1, /device:TPU:1, one launch (start us, length us, event | category | flops | bytes accessed | tf_op | source)
XLA Modules:
  0.0 473.8 jit_solution(18293331227726211427)
XLA Ops:
  51.0 25.3 %collective-permute-done.4 = bf16[192,768]{1,0:T(8,128)(2,1)} collective-permute-done((bf16[192,768]{1,0:T(8,128)(2,1)}, bf16[192,768]{1,0:T(8,128)(2,1)}, u32[]{:S(2)}, u32[]{:S(2)}) %collective-permute-start.4) | collective-permute-done | bytes 294944 | tf_op jit(solution)/shard_map/ppermute | solution.py:203
  76.3 3.3 collective-permute-start.5
  88.0 13.6 %collective-permute-done.8 = bf16[768,768]{1,0:T(8,128)(2,1)} collective-permute-done((bf16[768,768]{1,0:T(8,128)(2,1)S(1)}, bf16[768,768]{1,0:T(8,128)(2,1)}, u32[]{:S(2)}, u32[]{:S(2)}) %collective-permute-start.8) | collective-permute-done | bytes 1179680 | tf_op jit(solution)/shard_map/ppermute | solution.py:203
  101.6 3.3 collective-permute-start.9
  108.3 6.9 %add_convert_fusion.q_ref.k_ref.v_ref = bf16[768,2304]{1,0:T(8,128)(2,1)} fusion(bf16[768,2304]{1,0:T(8,128)(2,1)} %constant_dynamic-update-slice_fusion.37, f32[2304]{0:T(1024)S(1)} %fusion.21, bf16[384,768]{0,1:T(8,128)(2,1)} %collective-permute-done, bf16[384,768]{0,1:T(8,128)(2,1)S(1)} %bitcast.113), kind=kOutput, calls=%fused_computation.11 | convolution fusion | flops 2723807232 | bytes 8266752 | tf_op jit(solution)/shard_map/dot_general | solution.py:23
  115.2 18.5 %attention_forward.1 = (bf16[768,768]{1,0:T(8,128)(2,1)}, f32[768,768]{1,0:T(8,128)}) custom-call(bf16[768,2304]{1,0:T(8,128)(2,1)} %add_convert_fusion.q_ref.k_ref.v_ref, bf16[768,2304]{1,0:T(8,128)(2,1)} %add_convert_fusion.q_ref.k_ref.v_ref, bf16[768,2304]{1,0:T(8,128)(2,1)} %add_convert_fusion.q_ref.k_ref.v_ref, ...), custom_call_target="tpu_custom_call" | custom-call | flops 7247757312 | bytes 9437184 | tf_op jit(solution)/shard_map/attention_forward/pallas_call | solution.py:137
  133.7 3.4 fusion.39
  138.9 7.8 %multiply_convert_fusion = (bf16[768,3072]{1,0:T(8,128)(2,1)}, f32[768,3072]{1,0:T(8,128)S(1)}) fusion(f32[3072]{0:T(1024)S(1)} %copy-done.44, bf16[768,3072]{1,0:T(8,128)(2,1)S(1)} %constant_dynamic-update-slice_fusion.29, f32[768,768]{0,1:T(8,128)S(1)} %get-tuple-element.89, f32[768]{0:T(1024)S(1)} %add.470, f32[768]{0:T(1024)S(1)} %mul.289, ...), kind=kOutput, calls=%fused_computation.8 | convolution fusion | flops 3640983552 | bytes 21258240 | tf_op jit(solution)/shard_map/dot_general | solution.py:23
  149.1 7.9 %fusion.40 = (f32[768]{0:T(1024)S(1)}, f32[768,768]{0,1:T(8,128)S(1)}) fusion(f32[768]{0:T(1024)S(1)} %copy-done.54, bf16[768,3072]{1,0:T(8,128)(2,1)} %get-tuple-element.90, bf16[3072,768]{1,0:T(8,128)(2,1)} %constant_dynamic-update-slice_fusion.26, f32[768]{0:T(1024)S(1)} %add.470, f32[768]{0:T(1024)S(1)} %mul.289, f32[768]{0:T(1024)S(1)} %add_rsqrt_fusion.1, ...), kind=kOutput, calls=%fused_computation.215 | convolution fusion | flops 3628006656 | bytes 14174208 | tf_op jit(solution)/shard_map/dot_general | solution.py:23
  162.2 10.7 %convert_reduce_fusion = (f32[3072]{0:T(1024)}, bf16[768,3072]{1,0:T(8,128)(2,1)}) fusion(f32[768,3072]{1,0:T(8,128)S(1)} %get-tuple-element.91, f32[3072]{0:T(1024)S(1)} %copy-done.44, bf16[768,768]{0,1:T(8,128)(2,1)S(1)} %get-tuple-element.58, bf16[3072,768]{1,0:T(8,128)(2,1)} %constant_dynamic-update-slice_fusion.26), kind=kOutput, calls=%fused_computation.7 | convolution fusion | flops 3654546432 | bytes 20078592 | tf_op jit(solution)/shard_map/dot_general | solution.py:27
  172.9 8.1 %multiply_reduce_fusion.1 = (f32[768]{0:T(1024)}, f32[768]{0:T(1024)S(1)}, f32[768]{0:T(1024)S(1)}, f32[768]{0:T(1024)}, f32[768,768]{0,1:T(8,128)S(1)}) fusion(f32[768,768]{0,1:T(8,128)S(1)} %get-tuple-element.89, f32[768]{0:T(1024)S(1)} %add_rsqrt_fusion.1, f32[768]{0:T(1024)S(1)} %broadcast_multiply_fusion.5, f32[768]{0:T(1024)S(1)} %copy-done.38, ...), kind=kOutput, calls=%fused_computation.28 | convolution fusion | flops 3636851712 | bytes 17734656 | tf_op jit(solution)/shard_map/dot_general | solution.py:27
  184.4 26.3 %attention_backward.1 = (bf16[768,768]{1,0:T(8,128)(2,1)}, bf16[768,768]{1,0:T(8,128)(2,1)}, bf16[768,768]{1,0:T(8,128)(2,1)}) custom-call(bf16[768,2304]{1,0:T(8,128)(2,1)} %add_convert_fusion.q_ref.k_ref.v_ref, bf16[768,2304]{1,0:T(8,128)(2,1)} %add_convert_fusion.q_ref.k_ref.v_ref, bf16[768,2304]{1,0:T(8,128)(2,1)} %add_convert_fusion.q_ref.k_ref.v_ref, ...), custom_call_target="tpu_custom_call" | custom-call | flops 18119393280 | bytes 18874368 | tf_op jit(solution)/shard_map/attention_backward/pallas_call | solution.py:162
  213.1 4.0 fusion.27
  217.1 9.0 %fusion.30 = f32[768,3072]{1,0:T(8,128)} fusion(bf16[768,3072]{1,0:T(8,128)(2,1)} %get-tuple-element.96, f32[768,768]{0,1:T(8,128)S(1)} %get-tuple-element.89, f32[768]{0:T(1024)S(1)} %copy-done.53, f32[768]{0:T(1024)S(1)} %copy-done.39, f32[768]{0:T(1024)S(1)} %copy-done.41, f32[768]{0:T(1024)S(1)} %broadcast_multiply_fusion.5), kind=kOutput, calls=%fused_computation.209 | convolution fusion | flops 3626827776 | bytes 16527360 | tf_op jit(solution)/shard_map/dot_general | solution.py:31
  226.1 6.3 %fusion.41 = f32[3072,768]{1,0:T(8,128)} fusion(bf16[768,3072]{1,0:T(8,128)(2,1)S(1)} %bitcast.120, bf16[768,768]{0,1:T(8,128)(2,1)S(1)} %copy-done.26), kind=kOutput, calls=%fused_computation.216 | convolution fusion | flops 3623878656 | bytes 15335424 | tf_op jit(solution)/shard_map/dot_general | solution.py:31
  234.7 6.2 %add_convert_fusion.1 = bf16[768,768]{0,1:T(8,128)(2,1)S(1)} fusion(f32[768,768]{0,1:T(8,128)S(1)} %copy-done.16, bf16[768,2304]{1,0:T(8,128)(2,1)S(1)} %constant_dynamic-update-slice_fusion.43, bf16[768,2304]{1,0:T(8,128)(2,1)} %constant_dynamic-update-slice_fusion.37), kind=kOutput, calls=%fused_computation.32 | convolution fusion | flops 2719088640 | bytes 10616832 | tf_op jit(solution)/shard_map/dot_general | solution.py:27
  249.6 3.7 concatenate.99
  253.3 5.4 %fusion.17 = f32[768,2304]{1,0:T(8,128)S(1)} fusion(bf16[768,2304]{1,0:T(8,128)(2,1)} %copy-done.32, bf16[384,768]{0,1:T(8,128)(2,1)} %collective-permute-done, bf16[384,768]{0,1:T(8,128)(2,1)} %bitcast.112), kind=kOutput, calls=%fused_computation.92 | convolution fusion | flops 2720268288 | bytes 11796480 | tf_op jit(solution)/shard_map/dot_general | solution.py:31
  261.0 7.7 %collective-permute-done.23 = bf16[192,768]{1,0:T(8,128)(2,1)S(1)} collective-permute-done((bf16[192,768]{1,0:T(8,128)(2,1)S(1)}, bf16[192,768]{1,0:T(8,128)(2,1)S(1)}, u32[]{:S(2)}, u32[]{:S(2)}) %collective-permute-start.23) | collective-permute-done | bytes 294944 | tf_op jit(solution)/shard_map/ppermute | solution.py:203
  274.9 4.1 fusion.6
  289.1 4.5 collective-permute-done.27
  315.2 7.5 %collective-permute-done.14 = bf16[192,2432]{1,0:T(8,128)(2,1)} collective-permute-done((bf16[192,2432]{1,0:T(8,128)(2,1)}, bf16[192,2432]{1,0:T(8,128)(2,1)}, u32[]{:S(2)}, u32[]{:S(2)}) %collective-permute-start.14) | collective-permute-done | bytes 933920 | tf_op jit(solution)/shard_map/ppermute | solution.py:203
  324.5 3.9 bitcast_add_fusion.1
  328.8 4.6 collective-permute-done.15
  339.0 13.6 %collective-permute-done.32 = bf16[192,3072]{1,0:T(8,128)(2,1)S(1)} collective-permute-done((bf16[192,3072]{1,0:T(8,128)(2,1)S(1)}, bf16[192,3072]{1,0:T(8,128)(2,1)S(1)}, u32[]{:S(2)}, u32[]{:S(2)}) %collective-permute-start.32) | collective-permute-done | bytes 1179680 | tf_op jit(solution)/shard_map/ppermute | solution.py:203
  354.7 23.2 %collective-permute-done.41 = bf16[768,768]{1,0:T(8,128)(2,1)S(1)} collective-permute-done((bf16[768,768]{1,0:T(8,128)(2,1)S(1)}, bf16[768,768]{1,0:T(8,128)(2,1)S(1)}, u32[]{:S(2)}, u32[]{:S(2)}) %collective-permute-start.41) | collective-permute-done | bytes 1179680 | tf_op jit(solution)/shard_map/ppermute | solution.py:203
  385.6 6.3 %collective-permute-done.19 = bf16[48,2432]{1,0:T(8,128)(2,1)S(1)} collective-permute-done((bf16[48,2432]{1,0:T(8,128)(2,1)S(1)}, bf16[48,2432]{1,0:T(8,128)(2,1)S(1)}, u32[]{:S(2)}, u32[]{:S(2)}) %collective-permute-start.19) | collective-permute-done | bytes 233504 | tf_op jit(solution)/shard_map/ppermute | solution.py:203
  404.5 10.0 %collective-permute-start.21 = (bf16[192,2432]{1,0:T(8,128)(2,1)S(1)}, bf16[192,2432]{1,0:T(8,128)(2,1)S(1)}, u32[]{:S(2)}, u32[]{:S(2)}) collective-permute-start(bf16[192,2432]{1,0:T(8,128)(2,1)S(1)} %constant_dynamic-update-slice_fusion.18), channel_id=1, source_target_pairs={{0,2},{2,0},{4,6},{6,4},{8,10},{10,8},{12,14},{14,12},{16,18},{18,... | collective-permute-start | bytes 2801672 | tf_op jit(solution)/shard_map/ppermute | solution.py:203
  417.4 10.2 %collective-permute-done.36 = bf16[48,1536]{1,0:T(8,128)(2,1)S(1)} collective-permute-done((bf16[48,1536]{1,0:T(8,128)(2,1)S(1)}, bf16[48,1536]{1,0:T(8,128)(2,1)S(1)}, u32[]{:S(2)}, u32[]{:S(2)}) %collective-permute-start.36) | collective-permute-done | bytes 147488 | tf_op jit(solution)/shard_map/ppermute | solution.py:203
  427.6 4.5 collective-permute-done.45
  437.7 4.8 %collective-permute-done.46 = bf16[192,768]{1,0:T(8,128)(2,1)S(1)} collective-permute-done((bf16[192,768]{1,0:T(8,128)(2,1)S(1)}, bf16[192,768]{1,0:T(8,128)(2,1)S(1)}, u32[]{:S(2)}, u32[]{:S(2)}) %collective-permute-start.46) | collective-permute-done | bytes 294944 | tf_op jit(solution)/shard_map/ppermute | solution.py:203
  446.1 12.5 %collective-permute-start.39 = (bf16[192,3072]{1,0:T(8,128)(2,1)S(1)}, bf16[192,3072]{1,0:T(8,128)(2,1)}, u32[]{:S(2)}, u32[]{:S(2)}) collective-permute-start(bf16[192,3072]{1,0:T(8,128)(2,1)S(1)} %constant_dynamic-update-slice_fusion.6), channel_id=1, source_target_pairs={{0,2},{2,0},{4,6},{6,4},{8,10},{10,8},{12,14},{14,12},{16,18},{18,... | collective-permute-start | bytes 3538952 | tf_op jit(solution)/shard_map/ppermute | solution.py:203
  (407 shorter events, 183.9 us)
Async XLA Ops:
  7.0 39.1 %collective-permute-start.3 = (bf16[16,384]{1,0:T(8,128)(2,1)S(1)}, bf16[16,384]{1,0:T(8,128)(2,1)}, u32[]{:S(2)}, u32[]{:S(2)}) collective-permute-start(bf16[16,384]{1,0:T(8,128)(2,1)S(1)} %concatenate.83), channel_id=1, source_target_pairs={{0,1},{1,0},{2,3},{3,2},{4,5},{5,4},{6,7},{7,6},{8,9},{9,8},{10,11... | collective-permute-start | bytes 36872 | tf_op jit(solution)/shard_map/ppermute | solution.py:203
  11.6 73.6 %collective-permute-start.6 = (bf16[192,3072]{1,0:T(8,128)(2,1)}, bf16[192,3072]{1,0:T(8,128)(2,1)}, u32[]{:S(2)}, u32[]{:S(2)}) collective-permute-start(bf16[192,3072]{1,0:T(8,128)(2,1)} %constant_dynamic-slice_fusion.3), channel_id=1, source_target_pairs={{0,1},{1,0},{2,3},{3,2},{4,5},{5,4},{6,7},{7,6},{8,9},{9,8},{10,11... | collective-permute-start | bytes 3538952 | tf_op jit(solution)/shard_map/ppermute | solution.py:203
  12.8 69.4 %collective-permute-start.1 = (bf16[192,2304]{1,0:T(8,128)(2,1)}, bf16[192,2304]{1,0:T(8,128)(2,1)}, u32[]{:S(2)}, u32[]{:S(2)}) collective-permute-start(bf16[192,2304]{1,0:T(8,128)(2,1)} %constant_dynamic-slice_fusion.8), channel_id=1, source_target_pairs={{0,1},{1,0},{2,3},{3,2},{4,5},{5,4},{6,7},{7,6},{8,9},{9,8},{10,11... | collective-permute-start | bytes 2654216 | tf_op jit(solution)/shard_map/ppermute | solution.py:203
  18.9 89.4 %collective-permute-start = (bf16[384,768]{0,1:T(8,128)(2,1)}, bf16[384,768]{0,1:T(8,128)(2,1)}, u32[]{:S(2)}, u32[]{:S(2)}) collective-permute-start(bf16[384,768]{0,1:T(8,128)(2,1)} %bitcast.110), channel_id=1, source_target_pairs={{0,1},{1,0},{2,3},{3,2},{4,5},{5,4},{6,7},{7,6},{8,9},{9,8},{10,11... | collective-permute-start | bytes 1769480 | tf_op jit(solution)/shard_map/ppermute | solution.py:282
  20.6 55.7 %collective-permute-start.4 = (bf16[192,768]{1,0:T(8,128)(2,1)}, bf16[192,768]{1,0:T(8,128)(2,1)}, u32[]{:S(2)}, u32[]{:S(2)}) collective-permute-start(bf16[192,768]{1,0:T(8,128)(2,1)} %constant_dynamic-slice_fusion.4), channel_id=1, source_target_pairs={{0,1},{1,0},{2,3},{3,2},{4,5},{5,4},{6,7},{7,6},{8,9},{9,8},{10,11... | collective-permute-start | bytes 884744 | tf_op jit(solution)/shard_map/ppermute | solution.py:203
  46.1 55.4 %collective-permute-start.8 = (bf16[768,768]{1,0:T(8,128)(2,1)S(1)}, bf16[768,768]{1,0:T(8,128)(2,1)}, u32[]{:S(2)}, u32[]{:S(2)}) collective-permute-start(bf16[768,768]{1,0:T(8,128)(2,1)S(1)} %constant_dynamic-slice_fusion.2), channel_id=1, source_target_pairs={{0,1},{1,0},{2,3},{3,2},{4,5},{5,4},{6,7},{7,6},{8,9},{9,8},{10,11... | collective-permute-start | bytes 3538952 | tf_op jit(solution)/shard_map/ppermute | solution.py:203
  82.2 75.2 %collective-permute-start.11 = (bf16[384,768]{0,1:T(8,128)(2,1)}, bf16[384,768]{0,1:T(8,128)(2,1)S(1)}, u32[]{:S(2)}, u32[]{:S(2)}) collective-permute-start(bf16[384,768]{0,1:T(8,128)(2,1)} %bitcast.114), channel_id=1, source_target_pairs={{0,1},{1,0},{2,3},{3,2},{4,5},{5,4},{6,7},{7,6},{8,9},{9,8},{10,11... | collective-permute-start | bytes 1769480 | tf_op jit(solution)/shard_map/ppermute | solution.py:282
  82.2 25.1 %collective-permute-start.2 = (bf16[192,2304]{1,0:T(8,128)(2,1)}, bf16[192,2304]{1,0:T(8,128)(2,1)S(1)}, u32[]{:S(2)}, u32[]{:S(2)}) collective-permute-start(bf16[192,2304]{1,0:T(8,128)(2,1)} %collective-permute-done.1), channel_id=1, source_target_pairs={{0,2},{2,0},{4,6},{6,4},{8,10},{10,8},{12,14},{14,12},{16,18},{18,... | collective-permute-start | bytes 2654216 | tf_op jit(solution)/shard_map/ppermute | solution.py:203
  85.2 52.2 %collective-permute-start.7 = (bf16[192,3072]{1,0:T(8,128)(2,1)}, bf16[192,3072]{1,0:T(8,128)(2,1)}, u32[]{:S(2)}, u32[]{:S(2)}) collective-permute-start(bf16[192,3072]{1,0:T(8,128)(2,1)} %collective-permute-done.6), channel_id=1, source_target_pairs={{0,2},{2,0},{4,6},{6,4},{8,10},{10,8},{12,14},{14,12},{16,18},{18,... | collective-permute-start | bytes 3538952 | tf_op jit(solution)/shard_map/ppermute | solution.py:203
  101.6 45.1 %collective-permute-start.9 = (bf16[768,768]{1,0:T(8,128)(2,1)}, bf16[768,768]{1,0:T(8,128)(2,1)}, u32[]{:S(2)}, u32[]{:S(2)}) collective-permute-start(bf16[768,768]{1,0:T(8,128)(2,1)} %collective-permute-done.8), channel_id=1, source_target_pairs={{0,2},{2,0},{4,6},{6,4},{8,10},{10,8},{12,14},{14,12},{16,18},{18,... | collective-permute-start | bytes 3538952 | tf_op jit(solution)/shard_map/ppermute | solution.py:203
  233.6 73.5 %collective-permute-start.10 = (bf16[384,768]{0,1:T(8,128)(2,1)}, bf16[384,768]{0,1:T(8,128)(2,1)}, u32[]{:S(2)}, u32[]{:S(2)}) collective-permute-start(bf16[384,768]{0,1:T(8,128)(2,1)} %get-tuple-element.76), channel_id=1, source_target_pairs={{1,0},{0,1},{3,2},{2,3},{5,4},{4,5},{7,6},{6,7},{9,8},{8,9},{11,10... | collective-permute-start | bytes 1769480 | tf_op jit(solution)/shard_map/ppermute | solution.py:295
  242.2 67.3 %collective-permute-start.12 = (bf16[384,768]{0,1:T(8,128)(2,1)}, bf16[384,768]{0,1:T(8,128)(2,1)}, u32[]{:S(2)}, u32[]{:S(2)}) collective-permute-start(bf16[384,768]{0,1:T(8,128)(2,1)} %get-tuple-element.72), channel_id=1, source_target_pairs={{1,0},{0,1},{3,2},{2,3},{5,4},{4,5},{7,6},{6,7},{9,8},{8,9},{11,10... | collective-permute-start | bytes 1769480 | tf_op jit(solution)/shard_map/ppermute | solution.py:295
  248.2 10.5 %collective-permute-start.22 = (bf16[2,192,768]{2,1,0:T(8,128)(2,1)}, bf16[2,192,768]{2,1,0:T(8,128)(2,1)}, u32[]{:S(2)}, u32[]{:S(2)}) collective-permute-start(bf16[2,192,768]{2,1,0:T(8,128)(2,1)} %fusion.16), channel_id=1, source_target_pairs={{0,2},{2,0},{4,6},{6,4},{8,10},{10,8},{12,14},{14,12},{16,18},{18,... | collective-permute-start | bytes 1769480 | tf_op jit(solution)/shard_map/ppermute | solution.py:203
  271.6 26.7 %collective-permute-start.13 = (bf16[2,192,2432]{2,1,0:T(8,128)(2,1)}, bf16[2,192,2432]{2,1,0:T(8,128)(2,1)}, u32[]{:S(2)}, u32[]{:S(2)}) collective-permute-start(bf16[2,192,2432]{2,1,0:T(8,128)(2,1)} %fusion.12), channel_id=1, source_target_pairs={{0,2},{2,0},{4,6},{6,4},{8,10},{10,8},{12,14},{14,12},{16,18},{18,... | collective-permute-start | bytes 5603336 | tf_op jit(solution)/shard_map/ppermute | solution.py:203
  279.0 45.5 %collective-permute-start.31 = (bf16[2,192,3072]{2,1,0:T(8,128)(2,1)}, bf16[2,192,3072]{2,1,0:T(8,128)(2,1)}, u32[]{:S(2)}, u32[]{:S(2)}) collective-permute-start(bf16[2,192,3072]{2,1,0:T(8,128)(2,1)} %fusion.6), channel_id=1, source_target_pairs={{0,2},{2,0},{4,6},{6,4},{8,10},{10,8},{12,14},{14,12},{16,18},{18,... | collective-permute-start | bytes 7077896 | tf_op jit(solution)/shard_map/ppermute | solution.py:203
  302.3 20.4 %collective-permute-start.14 = (bf16[192,2432]{1,0:T(8,128)(2,1)}, bf16[192,2432]{1,0:T(8,128)(2,1)}, u32[]{:S(2)}, u32[]{:S(2)}) collective-permute-start(bf16[192,2432]{1,0:T(8,128)(2,1)} %fusion.15), channel_id=1, source_target_pairs={{0,1},{1,0},{2,3},{3,2},{4,5},{5,4},{6,7},{7,6},{8,9},{9,8},{10,11... | collective-permute-start | bytes 2801672 | tf_op jit(solution)/shard_map/ppermute | solution.py:203
  307.2 26.7 %collective-permute-start.40 = (bf16[2,768,768]{2,1,0:T(8,128)(2,1)S(1)}, bf16[2,768,768]{2,1,0:T(8,128)(2,1)}, u32[]{:S(2)}, u32[]{:S(2)}) collective-permute-start(bf16[2,768,768]{2,1,0:T(8,128)(2,1)S(1)} %fusion.7), channel_id=1, source_target_pairs={{0,2},{2,0},{4,6},{6,4},{8,10},{10,8},{12,14},{14,12},{16,18},{18,... | collective-permute-start | bytes 7077896 | tf_op jit(solution)/shard_map/ppermute | solution.py:203
  328.5 24.0 %collective-permute-start.32 = (bf16[192,3072]{1,0:T(8,128)(2,1)S(1)}, bf16[192,3072]{1,0:T(8,128)(2,1)S(1)}, u32[]{:S(2)}, u32[]{:S(2)}) collective-permute-start(bf16[192,3072]{1,0:T(8,128)(2,1)S(1)} %fusion.13), channel_id=1, source_target_pairs={{0,1},{1,0},{2,3},{3,2},{4,5},{5,4},{6,7},{7,6},{8,9},{9,8},{10,11... | collective-permute-start | bytes 3538952 | tf_op jit(solution)/shard_map/ppermute | solution.py:203
  336.3 41.6 %collective-permute-start.41 = (bf16[768,768]{1,0:T(8,128)(2,1)S(1)}, bf16[768,768]{1,0:T(8,128)(2,1)S(1)}, u32[]{:S(2)}, u32[]{:S(2)}) collective-permute-start(bf16[768,768]{1,0:T(8,128)(2,1)S(1)} %fusion.14), channel_id=1, source_target_pairs={{0,1},{1,0},{2,3},{3,2},{4,5},{5,4},{6,7},{7,6},{8,9},{9,8},{10,11... | collective-permute-start | bytes 3538952 | tf_op jit(solution)/shard_map/ppermute | solution.py:203
  338.9 39.2 %collective-permute-start.17 = (bf16[48,1216]{1,0:T(8,128)(2,1)S(1)}, bf16[48,1216]{1,0:T(8,128)(2,1)S(1)}, u32[]{:S(2)}, u32[]{:S(2)}) collective-permute-start(bf16[48,1216]{1,0:T(8,128)(2,1)S(1)} %dynamic-slice_convert_fusion.13), channel_id=1, source_target_pairs={{0,16},{2,18},{4,20},{6,22},{8,24},{10,26},{12,28},{14,30},{16,0},... | collective-permute-start | bytes 350216 | tf_op jit(solution)/shard_map/ppermute | solution.py:203
  352.9 40.8 %collective-permute-start.33 = (bf16[96,3072]{1,0:T(8,128)(2,1)S(1)}, bf16[96,3072]{1,0:T(8,128)(2,1)}, u32[]{:S(2)}, u32[]{:S(2)}) collective-permute-start(bf16[96,3072]{1,0:T(8,128)(2,1)S(1)} %dynamic-slice_convert_fusion.4), channel_id=1, source_target_pairs={{0,4},{2,6},{4,0},{6,2},{8,12},{10,14},{12,8},{14,10},{16,20},{18,... | collective-permute-start | bytes 1769480 | tf_op jit(solution)/shard_map/ppermute | solution.py:203
  380.4 14.9 %collective-permute-start.42 = (bf16[384,768]{1,0:T(8,128)(2,1)}, bf16[384,768]{1,0:T(8,128)(2,1)}, u32[]{:S(2)}, u32[]{:S(2)}) collective-permute-start(bf16[384,768]{1,0:T(8,128)(2,1)} %dynamic-slice_convert_fusion.3), channel_id=1, source_target_pairs={{0,4},{2,6},{4,0},{6,2},{8,12},{10,14},{12,8},{14,10},{16,20},{18,... | collective-permute-start | bytes 1769480 | tf_op jit(solution)/shard_map/ppermute | solution.py:203
  391.9 12.5 %collective-permute-start.20 = (bf16[96,2432]{1,0:T(8,128)(2,1)S(1)}, bf16[96,2432]{1,0:T(8,128)(2,1)S(1)}, u32[]{:S(2)}, u32[]{:S(2)}) collective-permute-start(bf16[96,2432]{1,0:T(8,128)(2,1)S(1)} %constant_dynamic-update-slice_fusion.20), channel_id=1, source_target_pairs={{0,4},{2,6},{4,0},{6,2},{8,12},{10,14},{12,8},{14,10},{16,20},{18,... | collective-permute-start | bytes 1400840 | tf_op jit(solution)/shard_map/ppermute | solution.py:203
  401.2 13.3 %collective-permute-start.35 = (bf16[48,1536]{1,0:T(8,128)(2,1)S(1)}, bf16[48,1536]{1,0:T(8,128)(2,1)S(1)}, u32[]{:S(2)}, u32[]{:S(2)}) collective-permute-start(bf16[48,1536]{1,0:T(8,128)(2,1)S(1)} %dynamic-slice_convert_fusion.11), channel_id=1, source_target_pairs={{0,16},{2,18},{4,20},{6,22},{8,24},{10,26},{12,28},{14,30},{16,0},... | collective-permute-start | bytes 442376 | tf_op jit(solution)/shard_map/ppermute | solution.py:203
  404.3 12.9 %collective-permute-start.44 = (bf16[96,768]{1,0:T(8,128)(2,1)S(1)}, bf16[96,768]{1,0:T(8,128)(2,1)S(1)}, u32[]{:S(2)}, u32[]{:S(2)}) collective-permute-start(bf16[96,768]{1,0:T(8,128)(2,1)S(1)} %dynamic-slice_convert_fusion.10), channel_id=1, source_target_pairs={{0,16},{2,18},{4,20},{6,22},{8,24},{10,26},{12,28},{14,30},{16,0},... | collective-permute-start | bytes 442376 | tf_op jit(solution)/shard_map/ppermute | solution.py:203
  404.5 54.2 %collective-permute-start.21 = (bf16[192,2432]{1,0:T(8,128)(2,1)S(1)}, bf16[192,2432]{1,0:T(8,128)(2,1)S(1)}, u32[]{:S(2)}, u32[]{:S(2)}) collective-permute-start(bf16[192,2432]{1,0:T(8,128)(2,1)S(1)} %constant_dynamic-update-slice_fusion.18), channel_id=1, source_target_pairs={{0,2},{2,0},{4,6},{6,4},{8,10},{10,8},{12,14},{14,12},{16,18},{18,... | collective-permute-start | bytes 2801672 | tf_op jit(solution)/shard_map/ppermute | solution.py:203
  414.5 13.0 %collective-permute-start.36 = (bf16[48,1536]{1,0:T(8,128)(2,1)S(1)}, bf16[48,1536]{1,0:T(8,128)(2,1)S(1)}, u32[]{:S(2)}, u32[]{:S(2)}) collective-permute-start(bf16[48,1536]{1,0:T(8,128)(2,1)S(1)} %get-tuple-element.54), channel_id=1, source_target_pairs={{0,16},{2,18},{4,20},{6,22},{8,24},{10,26},{12,28},{14,30},{16,0},... | collective-permute-start | bytes 442376 | tf_op jit(solution)/shard_map/ppermute | solution.py:203
  417.3 14.8 %collective-permute-start.45 = (bf16[96,768]{1,0:T(8,128)(2,1)S(1)}, bf16[96,768]{1,0:T(8,128)(2,1)S(1)}, u32[]{:S(2)}, u32[]{:S(2)}) collective-permute-start(bf16[96,768]{1,0:T(8,128)(2,1)S(1)} %get-tuple-element.52), channel_id=1, source_target_pairs={{0,16},{2,18},{4,20},{6,22},{8,24},{10,26},{12,28},{14,30},{16,0},... | collective-permute-start | bytes 442376 | tf_op jit(solution)/shard_map/ppermute | solution.py:203
  432.1 10.3 %collective-permute-start.46 = (bf16[192,768]{1,0:T(8,128)(2,1)S(1)}, bf16[192,768]{1,0:T(8,128)(2,1)S(1)}, u32[]{:S(2)}, u32[]{:S(2)}) collective-permute-start(bf16[192,768]{1,0:T(8,128)(2,1)S(1)} %constant_dynamic-update-slice_fusion.4), channel_id=1, source_target_pairs={{0,8},{2,10},{4,12},{6,14},{8,0},{10,2},{12,4},{14,6},{16,24},{18,... | collective-permute-start | bytes 884744 | tf_op jit(solution)/shard_map/ppermute | solution.py:203
  436.1 9.9 %collective-permute-start.38 = (bf16[96,3072]{1,0:T(8,128)(2,1)S(1)}, bf16[96,3072]{1,0:T(8,128)(2,1)S(1)}, u32[]{:S(2)}, u32[]{:S(2)}) collective-permute-start(bf16[96,3072]{1,0:T(8,128)(2,1)S(1)} %constant_dynamic-update-slice_fusion.8), channel_id=1, source_target_pairs={{0,4},{2,6},{4,0},{6,2},{8,12},{10,14},{12,8},{14,10},{16,20},{18,... | collective-permute-start | bytes 1769480 | tf_op jit(solution)/shard_map/ppermute | solution.py:203
  443.2 20.9 %collective-permute-start.47 = (bf16[384,768]{1,0:T(8,128)(2,1)}, bf16[384,768]{1,0:T(8,128)(2,1)}, u32[]{:S(2)}, u32[]{:S(2)}) collective-permute-start(bf16[384,768]{1,0:T(8,128)(2,1)} %constant_dynamic-update-slice_fusion.2), channel_id=1, source_target_pairs={{0,4},{2,6},{4,0},{6,2},{8,12},{10,14},{12,8},{14,10},{16,20},{18,... | collective-permute-start | bytes 1769480 | tf_op jit(solution)/shard_map/ppermute | solution.py:203
  446.1 20.3 %collective-permute-start.39 = (bf16[192,3072]{1,0:T(8,128)(2,1)S(1)}, bf16[192,3072]{1,0:T(8,128)(2,1)}, u32[]{:S(2)}, u32[]{:S(2)}) collective-permute-start(bf16[192,3072]{1,0:T(8,128)(2,1)S(1)} %constant_dynamic-update-slice_fusion.6), channel_id=1, source_target_pairs={{0,2},{2,0},{4,6},{6,4},{8,10},{10,8},{12,14},{14,12},{16,18},{18,... | collective-permute-start | bytes 3538952 | tf_op jit(solution)/shard_map/ppermute | solution.py:203
  (81 other events, 672.2 us)

commit v2 on v1

--- a/solution.py
+++ b/solution.py
@@ -297,7 +297,429 @@
     return out
 
 
-def body(
+def rows_at(start, size):
+    return pl.ds(pl.multiple_of(start, 16), size)
+
+
+def cols_at(start, size):
+    return pl.ds(pl.multiple_of(start, PAIR), size)
+
+
+class Here:
+    def __init__(self):
+        self.rep = lax.axis_index("rep")
+        self.y = lax.axis_index("shard")
+        self.core = lax.rem(self.rep, 2)
+        self.x = lax.rem(lax.div(self.rep, 2), 2)
+
+    def across(self, bit):
+        up = lax.rem(lax.div(self.rep, bit), 2)
+        return {"rep": self.rep + bit * (1 - 2 * up)}
+
+    def over(self):
+        return {"shard": 1 - self.y}
+
+
+class Copies:
+    def __init__(self, send, recv):
+        self.send, self.recv, self.used, self.open = send, recv, 0, []
+
+    def away(self, source, target, peer):
+        k = self.used
+        self.used += 1
+        copy = pltpu.make_async_remote_copy(
+            src_ref=source,
+            dst_ref=target,
+            send_sem=self.send.at[k],
+            recv_sem=self.recv.at[k],
+            device_id=peer,
+            device_id_type=pl.DeviceIdType.MESH,
+        )
+        return copy
+
+    def near(self, source, target):
+        k = self.used
+        self.used += 1
+        return pltpu.make_async_copy(source, target, self.recv.at[k])
+
+
+def greet(peers):
+    barrier = pltpu.get_barrier_semaphore()
+    for peer in peers:
+        pl.semaphore_signal(barrier, inc=1, device_id=peer, device_id_type=pl.DeviceIdType.MESH)
+    pl.semaphore_wait(barrier, len(peers))
+
+
+class Gathered:
+    def __init__(self, here, copies, own, full, cols):
+        n = own.shape[0]
+        h = n // 4
+        q = 2 * here.x + here.core
+        across = 2 * (1 - here.x) + here.core
+        mine, other = here.y * n, (1 - here.y) * n
+
+        def at(start, size):
+            return full.at[rows_at(start, size), cols]
+
+        self.local = copies.near(own, at(mine, n))
+        self.over = copies.away(own.at[rows_at(q * h, h), :], at(mine + q * h, h), here.over())
+        first, second = at(other + q * h, h), at(other + across * h, h)
+        self.side = copies.away(first, first, here.across(2))
+        self.core_one = copies.away(first, first, here.across(1))
+        self.core_two = copies.away(second, second, here.across(1))
+
+    def start(self):
+        self.over.start()
+        self.local.start()
+
+    def forward_one(self):
+        self.over.wait_recv()
+        self.side.start()
+        self.core_one.start()
+
+    def forward_two(self):
+        self.side.wait_recv()
+        self.core_two.start()
+
+    def ready(self):
+        self.local.wait()
+        self.core_one.wait_recv()
+        self.core_two.wait_recv()
+
+    def finish(self):
+        for copy in (self.over, self.side, self.core_one, self.core_two):
+            copy.wait_send()
+
+
+def gelu_parts(pre):
+    lower = 0.5 * (1.0 + lax.erf(pre * 0.7071067811865476))
+    density = jnp.exp(-0.5 * pre * pre) * 0.3989422804014327
+    return pre * lower, lower + pre * density
+
+
+def forward_kernel(
+    tokens,
+    cotangent,
+    seq,
+    vectors,
+    w_query,
+    w_key,
+    w_value,
+    w_attn,
+    w_up,
+    w_down,
+    o_x,
+    o_three,
+    o_attn,
+    o_up,
+    o_qkv,
+    o_heads,
+    o_lse,
+    o_normed,
+    o_inverse,
+    o_hidden,
+    o_active,
+    o_branch,
+    o_pre,
+    o_second,
+    o_layer,
+    o_sums,
+    o_sums_up,
+    x,
+    slope,
+    three,
+    proj,
+    up,
+    down,
+    raw_vectors,
+    vecs,
+    vec_up,
+    qkv,
+    heads,
+    lse,
+    mq,
+    mk,
+    normed,
+    inverse,
+    hidden,
+    active,
+    bend,
+    branch,
+    second,
+    layer,
+    sums,
+    sums_up,
+    send,
+    recv,
+):
+    here = Here()
+    copies = Copies(send, recv)
+    n = w_query.shape[0]
+    y = here.y
+    greet([here.over(), here.across(1), here.across(2)])
+
+    g_query = Gathered(here, copies, w_query, three, pl.ds(0, D))
+    g_key = Gathered(here, copies, w_key, three, pl.ds(D, D))
+    g_value = Gathered(here, copies, w_value, three, pl.ds(2 * D, D))
+    g_attn = Gathered(here, copies, w_attn, proj, pl.ds(0, D))
+    g_up = Gathered(here, copies, w_up, up, pl.ds(0, up.shape[1]))
+    g_down = Gathered(here, copies, w_down, down, pl.ds(0, D))
+    vec_away = copies.away(vectors, raw_vectors.at[y], here.over())
+    vec_near = copies.near(vectors, raw_vectors.at[y])
+    low, high = pl.ds(0, n), pl.ds(n, n)
+    x_away = copies.away(tokens.at[1 - y], x.at[high, :], here.over())
+    x_near = copies.near(tokens.at[y], x.at[low, :])
+    s_away = copies.away(cotangent.at[1 - y], slope.at[high, :], here.over())
+    s_near = copies.near(cotangent.at[y], slope.at[low, :])
+    for part in (g_query, g_key, g_value):
+        part.start()
+    vec_away.start()
+    vec_near.start()
+    x_away.start()
+    x_near.start()
+    for part in (g_attn, g_up, g_down):
+        part.start()
+    s_away.start()
+    s_near.start()
+
+    length = seq[y, 0]
+
+    def inside(start, size):
+        row = start + lax.broadcasted_iota(jnp.int32, (size, 1), 0)
+        place = row + jnp.where(row < n, y * n, -y * n)
+        return (place < length).astype(f32)
+
+    first = inside(0, 2 * n)
+    lane = lax.rem(lax.broadcasted_iota(jnp.int32, (1, PAIR), 1), DH)
+    mq[...] = jnp.where(
+        lane == 0, -BIG * first, jnp.where(lane == 1, -BIG * (1.0 - first), 0.0)
+    ).astype(bf16)
+    mk[...] = jnp.where(lane == 0, 1.0 - first, jnp.where(lane == 1, first, 0.0)).astype(bf16)
+
+    for part in (g_query, g_key, g_value):
+        part.forward_one()
+    for part in (g_query, g_key, g_value):
+        part.forward_two()
+    vec_away.wait_recv()
+    vec_near.wait()
+    for half in range(2):
+        table = raw_vectors[half].astype(f32)
+        vecs[:, half * n : (half + 1) * n] = table
+        wide = up.shape[1] // (2 * n)
+        for i in range(wide):
+            start = half * wide * n + i * n
+            vec_up[:, start : start + n] = table[8 + i : 9 + i, :]
+    for part in (g_query, g_key, g_value):
+        part.ready()
+    x_away.wait_recv()
+    x_near.wait()
+
+    tile = 256
+
+    @pl.loop(0, 3 * D // tile)
+    def _(i):
+        cols = cols_at(i * tile, tile)
+        which = lax.div(i, D // tile)
+        inner = cols_at(lax.rem(i, D // tile) * tile, tile)
+        bias = jnp.where(
+            which == 0, vecs[0:1, inner], jnp.where(which == 2, vecs[1:2, inner], 0.0)
+        )
+        qkv[:, cols] = (mm(x[...], three[:, cols]) + bias).astype(bf16)
+
+    lanes = lax.broadcasted_iota(jnp.int32, (1, PAIR), 1)
+    left = lanes < DH
+    lse[...] = jnp.zeros_like(lse)
+
+    @pl.loop(0, H * DH // PAIR)
+    def _(i):
+        keys, values = qkv[:, cols_at(D + i * PAIR, PAIR)], qkv[:, cols_at(2 * D + i * PAIR, PAIR)]
+        one = jnp.ones_like(values)
+        sides = []
+        for own in (left, jnp.logical_not(left)):
+            sides.append((own, jnp.where(own, keys, mk[...]), jnp.where(own, values, one)))
+        for start in range(0, 2 * n, ROWS):
+            rows = pl.ds(start, ROWS)
+            query = qkv[rows, cols_at(i * PAIR, PAIR)] * SCALE
+            outs = []
+            total_lse = lse[rows, :]
+            for side, (own, some_keys, some_values) in enumerate(sides):
+                scores = mm_nt(jnp.where(own, query, mq[rows, :]), some_keys)
+                top = jnp.max(scores, axis=1, keepdims=True)
+                expo = jnp.exp(scores - top).astype(bf16)
+                mixed = mm(expo, some_values)
+                total = pltpu.roll(mixed, DH, 1)
+                outs.append(mixed / total)
+                sum_all = jnp.where(own, total, mixed)
+                total_lse = jnp.where(lanes == 2 * i + side, top + jnp.log(sum_all), total_lse)
+            lse[rows, :] = total_lse
+            heads[rows, cols_at(i * PAIR, PAIR)] = jnp.where(left, outs[0], outs[1]).astype(bf16)
+
+        @pl.when(i == 0)
+        def _():
+            g_attn.forward_one()
+
+        @pl.when(i == 1)
+        def _():
+            g_attn.forward_two()
+
+        @pl.when(i == 3)
+        def _():
+            g_up.forward_one()
+
+        @pl.when(i == 5)
+        def _():
+            g_up.forward_two()
+
+    g_attn.ready()
+
+    @pl.loop(0, 2 * n // ROWS)
+    def _(i):
+        rows = rows_at(i * ROWS, ROWS)
+        resid = x[rows, :].astype(f32) + mm(heads[rows, :], proj[...]) + vecs[2:3, :]
+        some, scale = normalize(resid)
+        normed[rows, :] = some
+        inverse[rows, :] = jnp.broadcast_to(scale, (ROWS, PAIR))
+        hidden[rows, :] = (some * vecs[3:4, :] + vecs[4:5, :]).astype(bf16)
+
+    g_up.ready()
+    g_down.forward_one()
+
+    @pl.loop(0, up.shape[1] // tile)
+    def _(i):
+        cols = cols_at(i * tile, tile)
+        pre = mm(hidden[...], up[:, cols]) + vec_up[:, cols]
+        value, rate = gelu_parts(pre)
+        active[:, cols] = value.astype(bf16)
+        bend[:, cols] = rate.astype(bf16)
+
+        @pl.when(i == 6)
+        def _():
+            g_down.forward_two()
+
+    g_down.ready()
+    s_away.wait_recv()
+    s_near.wait()
+    sums[...] = jnp.zeros_like(sums)
+
+    @pl.loop(0, 2 * n // ROWS)
+    def _(i):
+        rows = rows_at(i * ROWS, ROWS)
+        resid = mm(active[rows, :], down[...]) + vecs[5:6, :]
+        resid = resid + (normed[rows, :] * vecs[3:4, :] + vecs[4:5, :])
+        some, scale = normalize(resid)
+        layer[rows, :] = (some * vecs[6:7, :] + vecs[7:8, :]).astype(bf16)
+        grad = slope[rows, :].astype(f32) * inside(i * ROWS, ROWS)
+        back = norm_back(grad, some, scale, vecs[6:7, :])
+        low_back = back.astype(bf16)
+        second[rows, :] = back
+        branch[rows, :] = low_back
+        sums[5:6, :] += jnp.sum(low_back.astype(f32), axis=0, keepdims=True)
+        sums[6:7, :] += jnp.sum(grad * some, axis=0, keepdims=True)
+        sums[7:8, :] += jnp.sum(grad, axis=0, keepdims=True)
+
+    @pl.loop(0, up.shape[1] // tile)
+    def _(i):
+        cols = cols_at(i * tile, tile)
+        rate = bend[:, cols].astype(f32)
+        low_pre = (mm_nt(branch[...], down[rows_at(i * tile, tile), :]) * rate).astype(bf16)
+        bend[:, cols] = low_pre
+        sums_up[:, cols] = jnp.sum(low_pre.astype(f32), axis=0, keepdims=True)
+
+    outs = [
+        copies.near(a, b)
+        for a, b in (
+            (x, o_x),
+            (three, o_three),
+            (proj, o_attn),
+            (up, o_up),
+            (qkv, o_qkv),
+            (heads, o_heads),
+            (lse, o_lse),
+            (normed, o_normed),
+            (inverse, o_inverse),
+            (hidden, o_hidden),
+            (active, o_active),
+            (branch, o_branch),
+            (bend, o_pre),
+            (second, o_second),
+            (layer, o_layer),
+            (sums, o_sums),
+            (sums_up, o_sums_up),
+        )
+    ]
+    for copy in outs:
+        copy.start()
+    for copy in outs:
+        copy.wait()
+    for part in (g_query, g_key, g_value, g_attn, g_up, g_down):
+        part.finish()
+    for copy in (vec_away, x_away, s_away):
+        copy.wait_send()
+
+
+def run_forward(tokens, cotangent, seq, vectors, weights):
+    n = weights[0].shape[0]
+    count, wide = 2 * n, weights[4].shape[1]
+    kinds = [
+        ((count, D), bf16),
+        ((D, 3 * D), bf16),
+        ((D, D), bf16),
+        ((D, wide), bf16),
+        ((count, 3 * D), bf16),
+        ((count, D), bf16),
+        ((count, PAIR), f32),
+        ((count, D), f32),
+        ((count, PAIR), f32),
+        ((count, D), bf16),
+        ((count, wide), bf16),
+        ((count, D), bf16),
+        ((count, wide), bf16),
+        ((count, D), f32),
+        ((count, D), bf16),
+        ((16, D), f32),
+        ((1, wide), f32),
+    ]
+    scratch = [
+        ((count, D), bf16),
+        ((count, D), bf16),
+        ((D, 3 * D), bf16),
+        ((D, D), bf16),
+        ((D, wide), bf16),
+        ((wide, D), bf16),
+        ((2, 16, n), bf16),
+        ((16, D), f32),
+        ((1, wide), f32),
+        ((count, 3 * D), bf16),
+        ((count, D), bf16),
+        ((count, PAIR), f32),
+        ((count, PAIR), bf16),
+        ((count, PAIR), bf16),
+        ((count, D), f32),
+        ((count, PAIR), f32),
+        ((count, D), bf16),
+        ((count, wide), bf16),
+        ((count, wide), bf16),
+        ((count, D), bf16),
+        ((count, D), f32),
+        ((count, D), bf16),
+        ((16, D), f32),
+        ((1, wide), f32),
+    ]
+    anywhere = pl.BlockSpec(memory_space=pl.ANY)
+    return pl.pallas_call(
+        forward_kernel,
+        out_shape=[jax.ShapeDtypeStruct(*kind) for kind in kinds],
+        in_specs=[anywhere, anywhere, pl.BlockSpec(memory_space=pltpu.SMEM)] + [anywhere] * 7,
+        out_specs=[anywhere] * len(kinds),
+        scratch_shapes=[pltpu.VMEM(*kind) for kind in scratch]
+        + [pltpu.SemaphoreType.DMA((64,)), pltpu.SemaphoreType.DMA((64,))],
+        compiler_params=pltpu.CompilerParams(
+            collective_id=0, has_side_effects=True, vmem_limit_bytes=66 * 1024 * 1024 - 3 * 1024 * 1024
+        ),
+        name="encoder_forward",
+    )(tokens, cotangent, seq, vectors, *weights)
+
+def general_body(
     tokens,
     cotangent,
     seq_lengths,
@@ -464,6 +886,121 @@
     )
 
 
+def body(tokens, cotangent, seq_lengths, *weights):
+    shards, micro = lax.axis_size("shard"), tokens.shape[0]
+    reps = lax.axis_size("rep")
+    if shards != 2 or micro != 2 or reps % 4:
+        return general_body(tokens, cotangent, seq_lengths, *weights)
+    (
+        w_query,
+        b_query,
+        w_key,
+        w_value,
+        b_value,
+        w_attn,
+        b_attn,
+        norm_gain,
+        norm_bias,
+        w_up,
+        b_up,
+        w_down,
+        b_down,
+        out_gain,
+        out_bias,
+    ) = weights
+    at = Places()
+    part = w_query.shape[0]
+    wide = b_up.shape[0] // part
+    vectors = jnp.concatenate(
+        [b_query, b_value, b_attn, norm_gain, norm_bias, b_down, out_gain, out_bias, b_up]
+        + [jnp.zeros(((8 - wide) * part,), bf16)]
+    ).reshape(16, part)
+    (
+        x,
+        w_three,
+        w_proj,
+        full_up,
+        three,
+        attn,
+        lse,
+        normed_one,
+        inverse_one,
+        hidden_low,
+        active,
+        grad_branch,
+        grad_pre,
+        grad_second,
+        layer,
+        sums,
+        d_up,
+    ) = run_forward(
+        tokens, cotangent, seq_lengths[:, 0], vectors, (w_query, w_key, w_value, w_attn, w_up, w_down)
+    )
+    slots = tokens.shape[1]
+    ids = segment_ids(lax.dynamic_index_in_dim(seq_lengths[:, 0], at.shard, 0, False), 2 * slots)
+    ids = jnp.roll(ids, -at.shard * slots)
+    mq, mk = mask_columns(ids)
+    base = D // PAIR
+    offsets = (base, 2 * base)
+    c_gain = None
+    table = put(jnp.zeros((2, part), bf16), norm_gain[None], at.shard)
+    there = swap(norm_gain[None], "shard", 2, lambda i: 1 - i)
+    c_gain = put(table, there, 1 - at.shard).reshape(1, D).astype(f32)
+    inverse_one = inverse_one[:, :1]
+    lse = jnp.repeat(lse[:, :H], DH, axis=1)
+    g_down = mm_tn(active, grad_branch)
+    g_up = mm_tn(hidden_low, grad_pre)
+    grad_hidden = mm_nt(grad_pre, full_up) + grad_second
+    d_gain = jnp.sum(grad_hidden * normed_one, axis=0)
+    d_bias = jnp.sum(grad_hidden, axis=0)
+    grad_first = norm_back(grad_hidden, normed_one, inverse_one, c_gain)
+    grad_proj = grad_first.astype(bf16)
+    d_attn = jnp.sum(grad_proj.astype(f32), axis=0)
+    g_attn = mm_tn(attn, grad_proj)
+    grad_attn = mm_nt(grad_proj, w_proj).astype(bf16)
+    dq, dk, dv = attention_backward(three, three, offsets, mq, mk, attn, lse, grad_attn)
+    d_three = jnp.concatenate([dq, dk, dv], axis=1)
+    d_query = jnp.sum(dq.astype(f32), axis=0)
+    d_value = jnp.sum(dv.astype(f32), axis=0)
+    g_three = mm_tn(x, d_three)
+    back = (grad_first + mm_nt(d_three, w_three)).astype(bf16)
+    sums = jnp.concatenate(
+        [
+            jnp.stack([d_query, d_value, d_attn, d_gain, d_bias, sums[5], sums[6], sums[7]]).reshape(
+                8, shards, part
+            ),
+            d_up.reshape(shards, wide, part).transpose(1, 0, 2),
+            jnp.zeros((PAIR - 8 - wide, shards, part), f32),
+        ],
+        axis=0,
+    )
+    sums = sums.reshape(PAIR, D).T
+    r_down = reduce_rows(at, g_down)
+    r_up = reduce_rows(at, g_up)
+    r_attn = reduce_rows(at, g_attn)
+    r_three = reduce_rows(at, jnp.concatenate([g_three, sums], axis=1))
+    small = r_three[:, 3 * D :].T
+    return (
+        collect(at, layer, micro),
+        collect(at, back, micro),
+        r_three[:, :D],
+        small[0],
+        r_three[:, D : 2 * D],
+        r_three[:, 2 * D : 3 * D],
+        small[1],
+        r_attn,
+        small[2],
+        small[3],
+        small[4],
+        r_up,
+        small[8 : 8 + wide].reshape(wide * part),
+        r_down,
+        small[5],
+        small[6],
+        small[7],
+    )
+
+
 def solution(mesh):
     rows, vector = P("shard", None), P("shard")
     tokens = P(None, ("rep", "shard"), None)

time: 482 us -> 429 us (0.89)
  Pallas kernels: 44.8 us -> 127 us
  local copies, waits for them, and re-layouts: 103 us -> 60.2 us
  waiting for transfers between devices: 142 us -> 100 us
  matrix products: 77.9 us -> 40.7 us
  other arithmetic: 40.1 us -> 31.8 us
    pallas_call x1, Pallas kernels: 18.5 us -> 101 us  [run_forward(): pl.pallas_call(forward_kernel, out_shape=[jax.ShapeDtypeStruct(*kind) for...]
    ppermute x45 -> x37, waiting for transfers between devices: 142 us -> 100 us  [swap(): return lax.ppermute(value, axis, [(i, move(i)) for i in range(size)])]
    dot_general x4 -> x0, matrix products: 26.1 us -> none  [mm(): return jnp.dot(left, right, preferred_element_type=f32)]
    dynamic_update_slice x35 -> x23, local copies, waits for them, and re-layouts: 26.9 us -> 8.33 us  [put(): lax.dynamic_update_slice_in_dim(buffer, value, index * value.shape[axis],...]
    dynamic_slice x11 -> x1, local copies, waits for them, and re-layouts: 14.2 us -> 0.01 us  [body(): lax.dynamic_index_in_dim(seq_lengths[:, 0], at.shard, 0, False)]
    dot_general x4 -> x3, matrix products: 27.1 us -> 14.5 us  [mm_nt(): lax.dot_general(left, right, (((1,), (1,)), ((), ())), preferred_element_...]
    broadcast_in_dim x10 -> x4, local copies, waits for them, and re-layouts: 9.89 us -> 0.76 us  [the longest x2 0.57 us: body(): table = put(jnp.zeros((2, part), bf16), norm_gain[None], at.shard)]
    unnamed x132 -> x89, local copies, waits for them, and re-layouts: 11.4 us -> 18 us
  transfers between devices with their start and end apart: 49 -> 39, of which waited for: 19 -> 18; matrix products, arithmetic and copies ran while one was open for 32% -> 26% of each run, Pallas kernels for 4% -> 6%
where the time goes in v2:
time: 429 us; the launch traced here: 423 us
  Pallas kernels  127 us (30%)
  waiting for transfers between devices  100 us (23%)
  starting transfers between devices  61.5 us (14%)
  local copies, waits for them, and re-layouts  60.2 us (14%)
  matrix products  40.7 us (9%)
  other arithmetic  31.8 us (7%)
    pallas_call x1, Pallas kernels, run_forward(): pl.pallas_call(forward_kernel, out_shape=[jax.ShapeDtypeStruct(*kind) for...  101 us
    ppermute x37, waiting for transfers between devices, swap(): return lax.ppermute(value, axis, [(i, move(i)) for i in range(size)])  100 us
    ppermute x37, starting transfers between devices, swap(): return lax.ppermute(value, axis, [(i, move(i)) for i in range(size)])  60.9 us
    dot_general x4, matrix products, mm_tn(): lax.dot_general(left, right, (((0,), (0,)), ((), ())), preferred_element_...  26.3 us
    pallas_call x1, Pallas kernels, attention_backward(): pl.pallas_call(backward_heads, grid=(pairs,), out_shape=(jax.ShapeDtypeSt...  26.1 us
    unnamed x89, local copies, waits for them, and re-layouts  18 us
    dot_general x3, matrix products, mm_nt(): lax.dot_general(left, right, (((1,), (1,)), ((), ())), preferred_element_...  14.5 us
  transfers between devices with their start and end apart: 39, of which 18 were waited for; matrix products, arithmetic and copies ran while one was open for 26% of the time, Pallas kernels for 6%

profile of v2, /device:TPU:1, one launch (start us, length us, event | category | flops | bytes accessed | tf_op | source)
XLA Modules:
  0.0 423.4 jit_solution(1050249993947221830)
XLA Ops:
  9.3 101.1 %encoder_forward.1 = (bf16[768,768]{1,0:T(8,128)(2,1)}, bf16[768,2304]{1,0:T(8,128)(2,1)}, bf16[768,768]{1,0:T(8,128)(2,1)}, bf16[768,3072]{1,0:T(8,128)(2,1)}, ...) custom-call(bf16[2,384,768]{2,1,0:T(8,128)(2,1)} %tokens.1, ...), custom_call_target="tpu_custom_call" | custom-call | tf_op jit(solution)/shard_map/encoder_forward/pallas_call | solution.py:709
  114.4 6.5 %fusion.14 = f32[768,3072]{1,0:T(8,128)S(1)} fusion(bf16[768,768]{1,0:T(8,128)(2,1)} %get-tuple-element.54, bf16[768,3072]{1,0:T(8,128)(2,1)} %get-tuple-element.39), kind=kOutput, calls=%fused_computation.133 | convolution fusion | flops 3623878656 | bytes 15335424 | tf_op jit(solution)/shard_map/dot_general | solution.py:31
  124.4 3.9 fusion.15
  128.3 3.6 copy-done.3
  151.8 9.4 %multiply_reduce_fusion = (f32[768]{0:T(1024)}, f32[768]{0:T(1024)S(1)}, f32[768]{0:T(1024)S(1)}, f32[768]{0:T(1024)}, f32[768,768]{1,0:T(8,128)S(1)}) fusion(f32[768,768]{1,0:T(8,128)S(1)} %copy-done.9, f32[768]{0:T(1024)S(1)} %reshape.162, f32[768,768]{1,0:T(8,128)} %get-tuple-element.41, bf16[768,3072]{1,0:T(8,128)(2,1)} %get-tuple-element.39, ...), kind=kOutput, calls=%fused_computation.15 | convolution fusion | flops 3628594176 | bytes 16530432 | tf_op jit(solution)/shard_map/dot_general | solution.py:27
  164.6 2.6 fusion.10
  167.2 26.1 %attention_backward.1 = (bf16[768,768]{1,0:T(8,128)(2,1)}, bf16[768,768]{1,0:T(8,128)(2,1)}, bf16[768,768]{1,0:T(8,128)(2,1)}) custom-call(bf16[768,2304]{1,0:T(8,128)(2,1)} %get-tuple-element.43.q_ref.k_ref.v_ref, bf16[768,2304]{1,0:T(8,128)(2,1)} %get-tuple-element.43.q_ref.k_ref.v_ref, bf16[768,2304]{1,0:T(8,128)(2,1)} %get-tuple-element.43.q_ref.k_ref.v_ref, ...), custom_call_target="tpu_custom_call" | custom-call | flops 18119393280 | bytes 18874368 | tf_op jit(solution)/shard_map/attention_backward/pallas_call | solution.py:162
  197.0 13.3 %fusion.13 = f32[768,2304]{1,0:T(8,128)} fusion(bf16[768,768]{1,0:T(8,128)(2,1)S(1)} %copy-done.13, bf16[768,2304]{1,0:T(8,128)(2,1)S(1)} %constant_dynamic-update-slice_fusion.22), kind=kOutput, calls=%fused_computation.132 | convolution fusion | flops 2717908992 | bytes 11796480 | tf_op jit(solution)/shard_map/dot_general | solution.py:31
  217.9 3.0 concatenate.56
  222.9 3.8 pad_maximum_fusion
  230.8 2.4 collective-permute-start.16
  233.2 3.0 add_convert_fusion
  237.2 2.8 collective-permute-done.17
  245.1 3.0 collective-permute-done.19
  249.3 6.4 %collective-permute-start.20 = (bf16[192,768]{1,0:T(8,128)(2,1)S(1)}, bf16[192,768]{1,0:T(8,128)(2,1)S(1)}, u32[]{:S(2)}, u32[]{:S(2)}) collective-permute-start(bf16[192,768]{1,0:T(8,128)(2,1)S(1)} %constant_dynamic-update-slice_fusion.12), channel_id=1, source_target_pairs={{0,2},{2,0},{4,6},{6,4},{8,10},{10,8},{12,14},{14,12},{16,18},{18,... | collective-permute-start | bytes 884744 | tf_op jit(solution)/shard_map/ppermute | solution.py:203
  258.8 15.1 %collective-permute-done.4 = bf16[192,2432]{1,0:T(8,128)(2,1)S(1)} collective-permute-done((bf16[192,2432]{1,0:T(8,128)(2,1)S(1)}, bf16[192,2432]{1,0:T(8,128)(2,1)S(1)}, u32[]{:S(2)}, u32[]{:S(2)}) %collective-permute-start.4) | collective-permute-done | bytes 933920 | tf_op jit(solution)/shard_map/ppermute | solution.py:203
  274.8 3.0 bitcast_add_fusion.1
  278.2 3.4 collective-permute-done.5
  287.8 11.8 %collective-permute-done.22 = bf16[192,3072]{1,0:T(8,128)(2,1)S(1)} collective-permute-done((bf16[192,3072]{1,0:T(8,128)(2,1)S(1)}, bf16[192,3072]{1,0:T(8,128)(2,1)S(1)}, u32[]{:S(2)}, u32[]{:S(2)}) %collective-permute-start.22) | collective-permute-done | bytes 1179680 | tf_op jit(solution)/shard_map/ppermute | solution.py:203
  301.1 23.8 %collective-permute-done.31 = bf16[768,768]{1,0:T(8,128)(2,1)S(1)} collective-permute-done((bf16[768,768]{1,0:T(8,128)(2,1)S(1)}, bf16[768,768]{1,0:T(8,128)(2,1)S(1)}, u32[]{:S(2)}, u32[]{:S(2)}) %collective-permute-start.31) | collective-permute-done | bytes 1179680 | tf_op jit(solution)/shard_map/ppermute | solution.py:203
  332.6 6.5 %collective-permute-done.9 = bf16[48,2432]{1,0:T(8,128)(2,1)S(1)} collective-permute-done((bf16[48,2432]{1,0:T(8,128)(2,1)S(1)}, bf16[48,2432]{1,0:T(8,128)(2,1)S(1)}, u32[]{:S(2)}, u32[]{:S(2)}) %collective-permute-start.9) | collective-permute-done | bytes 233504 | tf_op jit(solution)/shard_map/ppermute | solution.py:203
  344.6 4.5 %collective-permute-done.24 = bf16[48,3072]{1,0:T(8,128)(2,1)S(1)} collective-permute-done((bf16[48,3072]{1,0:T(8,128)(2,1)S(1)}, bf16[48,3072]{1,0:T(8,128)(2,1)S(1)}, u32[]{:S(2)}, u32[]{:S(2)}) %collective-permute-start.24) | collective-permute-done | bytes 294944 | tf_op jit(solution)/shard_map/ppermute | solution.py:203
  349.4 3.2 collective-permute-done.33
  352.9 11.9 %collective-permute-start.11 = (bf16[192,2432]{1,0:T(8,128)(2,1)S(1)}, bf16[192,2432]{1,0:T(8,128)(2,1)S(1)}, u32[]{:S(2)}, u32[]{:S(2)}) collective-permute-start(bf16[192,2432]{1,0:T(8,128)(2,1)S(1)} %constant_dynamic-update-slice_fusion.18), channel_id=1, source_target_pairs={{0,2},{2,0},{4,6},{6,4},{8,10},{10,8},{12,14},{14,12},{16,18},{18,... | collective-permute-start | bytes 2801672 | tf_op jit(solution)/shard_map/ppermute | solution.py:203
  367.4 9.2 %collective-permute-done.26 = bf16[48,1536]{1,0:T(8,128)(2,1)S(1)} collective-permute-done((bf16[48,1536]{1,0:T(8,128)(2,1)S(1)}, bf16[48,1536]{1,0:T(8,128)(2,1)S(1)}, u32[]{:S(2)}, u32[]{:S(2)}) %collective-permute-start.26) | collective-permute-done | bytes 147488 | tf_op jit(solution)/shard_map/ppermute | solution.py:203
  376.7 4.7 %collective-permute-done.35 = bf16[96,768]{1,0:T(8,128)(2,1)S(1)} collective-permute-done((bf16[96,768]{1,0:T(8,128)(2,1)S(1)}, bf16[96,768]{1,0:T(8,128)(2,1)S(1)}, u32[]{:S(2)}, u32[]{:S(2)}) %collective-permute-start.35) | collective-permute-done | bytes 147488 | tf_op jit(solution)/shard_map/ppermute | solution.py:203
  385.3 2.7 collective-permute-start.28
  388.0 3.5 collective-permute-done.36
  392.3 2.7 collective-permute-start.37
  396.5 11.4 %collective-permute-start.29 = (bf16[192,3072]{1,0:T(8,128)(2,1)S(1)}, bf16[192,3072]{1,0:T(8,128)(2,1)}, u32[]{:S(2)}, u32[]{:S(2)}) collective-permute-start(bf16[192,3072]{1,0:T(8,128)(2,1)S(1)} %constant_dynamic-update-slice_fusion.6), channel_id=1, source_target_pairs={{0,2},{2,0},{4,6},{6,4},{8,10},{10,8},{12,14},{14,12},{16,18},{18,... | collective-permute-start | bytes 3538952 | tf_op jit(solution)/shard_map/ppermute | solution.py:203
  417.7 2.8 maximum_convert_fusion
  420.6 2.5 maximum_convert_fusion.1
  (282 shorter events, 107.9 us)
Async XLA Ops:
  112.4 136.9 %collective-permute-start = (bf16[384,768]{1,0:T(8,128)(2,1)}, bf16[384,768]{1,0:T(8,128)(2,1)}, u32[]{:S(2)}, u32[]{:S(2)}) collective-permute-start(bf16[384,768]{1,0:T(8,128)(2,1)} %slice.68), channel_id=1, source_target_pairs={{1,0},{0,1},{3,2},{2,3},{5,4},{4,5},{7,6},{6,7},{9,8},{8,9},{11,10... | collective-permute-start | bytes 1769480 | tf_op jit(solution)/shard_map/ppermute | solution.py:295
  113.2 36.6 %collective-permute-start.1 = (bf16[1,384]{1,0:T(2,128)(2,1)}, bf16[1,384]{1,0:T(2,128)(2,1)}, u32[]{:S(2)}, u32[]{:S(2)}) collective-permute-start(bf16[1,384]{1,0:T(2,128)(2,1)} %broadcast_in_dim.125), channel_id=1, source_target_pairs={{0,1},{1,0},{2,3},{3,2},{4,5},{5,4},{6,7},{7,6},{8,9},{9,8},{10,11... | collective-permute-start | bytes 2312 | tf_op jit(solution)/shard_map/ppermute | solution.py:203
  122.6 152.2 %collective-permute-start.21 = (bf16[2,192,3072]{2,1,0:T(8,128)(2,1)}, bf16[2,192,3072]{2,1,0:T(8,128)(2,1)}, u32[]{:S(2)}, u32[]{:S(2)}) collective-permute-start(bf16[2,192,3072]{2,1,0:T(8,128)(2,1)} %fusion), channel_id=1, source_target_pairs={{0,2},{2,0},{4,6},{6,4},{8,10},{10,8},{12,14},{14,12},{16,18},{18,... | collective-permute-start | bytes 7077896 | tf_op jit(solution)/shard_map/ppermute | solution.py:203
  133.6 149.2 %collective-permute-start.30 = (bf16[2,768,768]{2,1,0:T(8,128)(2,1)}, bf16[2,768,768]{2,1,0:T(8,128)(2,1)}, u32[]{:S(2)}, u32[]{:S(2)}) collective-permute-start(bf16[2,768,768]{2,1,0:T(8,128)(2,1)} %fusion.1), channel_id=1, source_target_pairs={{0,2},{2,0},{4,6},{6,4},{8,10},{10,8},{12,14},{14,12},{16,18},{18,... | collective-permute-start | bytes 7077896 | tf_op jit(solution)/shard_map/ppermute | solution.py:203
  195.4 14.9 %collective-permute-start.12 = (bf16[2,192,768]{2,1,0:T(8,128)(2,1)S(1)}, bf16[2,192,768]{2,1,0:T(8,128)(2,1)S(1)}, u32[]{:S(2)}, u32[]{:S(2)}) collective-permute-start(bf16[2,192,768]{2,1,0:T(8,128)(2,1)S(1)} %fusion.6), channel_id=1, source_target_pairs={{0,2},{2,0},{4,6},{6,4},{8,10},{10,8},{12,14},{14,12},{16,18},{18,... | collective-permute-start | bytes 1769480 | tf_op jit(solution)/shard_map/ppermute | solution.py:203
  211.2 9.8 %collective-permute-start.13 = (bf16[192,768]{1,0:T(8,128)(2,1)}, bf16[192,768]{1,0:T(8,128)(2,1)}, u32[]{:S(2)}, u32[]{:S(2)}) collective-permute-start(bf16[192,768]{1,0:T(8,128)(2,1)} %fusion.8), channel_id=1, source_target_pairs={{0,1},{1,0},{2,3},{3,2},{4,5},{5,4},{6,7},{7,6},{8,9},{9,8},{10,11... | collective-permute-start | bytes 884744 | tf_op jit(solution)/shard_map/ppermute | solution.py:203
  229.0 15.0 %collective-permute-start.3 = (bf16[2,192,2432]{2,1,0:T(8,128)(2,1)S(1)}, bf16[2,192,2432]{2,1,0:T(8,128)(2,1)S(1)}, u32[]{:S(2)}, u32[]{:S(2)}) collective-permute-start(bf16[2,192,2432]{2,1,0:T(8,128)(2,1)S(1)} %fusion.2), channel_id=1, source_target_pairs={{0,2},{2,0},{4,6},{6,4},{8,10},{10,8},{12,14},{14,12},{16,18},{18,... | collective-permute-start | bytes 5603336 | tf_op jit(solution)/shard_map/ppermute | solution.py:203
  243.6 13.9 %collective-permute-start.2 = (bf16[384,768]{1,0:T(8,128)(2,1)S(1)}, bf16[384,768]{1,0:T(8,128)(2,1)S(1)}, u32[]{:S(2)}, u32[]{:S(2)}) collective-permute-start(bf16[384,768]{1,0:T(8,128)(2,1)S(1)} %slice.89), channel_id=1, source_target_pairs={{1,0},{0,1},{3,2},{2,3},{5,4},{4,5},{7,6},{6,7},{9,8},{8,9},{11,10... | collective-permute-start | bytes 1769480 | tf_op jit(solution)/shard_map/ppermute | solution.py:295
  248.1 25.8 %collective-permute-start.4 = (bf16[192,2432]{1,0:T(8,128)(2,1)S(1)}, bf16[192,2432]{1,0:T(8,128)(2,1)S(1)}, u32[]{:S(2)}, u32[]{:S(2)}) collective-permute-start(bf16[192,2432]{1,0:T(8,128)(2,1)S(1)} %fusion.5), channel_id=1, source_target_pairs={{0,1},{1,0},{2,3},{3,2},{4,5},{5,4},{6,7},{7,6},{8,9},{9,8},{10,11... | collective-permute-start | bytes 2801672 | tf_op jit(solution)/shard_map/ppermute | solution.py:203
  249.3 8.4 %collective-permute-start.20 = (bf16[192,768]{1,0:T(8,128)(2,1)S(1)}, bf16[192,768]{1,0:T(8,128)(2,1)S(1)}, u32[]{:S(2)}, u32[]{:S(2)}) collective-permute-start(bf16[192,768]{1,0:T(8,128)(2,1)S(1)} %constant_dynamic-update-slice_fusion.12), channel_id=1, source_target_pairs={{0,2},{2,0},{4,6},{6,4},{8,10},{10,8},{12,14},{14,12},{16,18},{18,... | collective-permute-start | bytes 884744 | tf_op jit(solution)/shard_map/ppermute | solution.py:203
  274.2 7.5 %collective-permute-start.5 = (bf16[96,2432]{1,0:T(8,128)(2,1)S(1)}, bf16[96,2432]{1,0:T(8,128)(2,1)S(1)}, u32[]{:S(2)}, u32[]{:S(2)}) collective-permute-start(bf16[96,2432]{1,0:T(8,128)(2,1)S(1)} %dynamic-slice_convert_fusion.5), channel_id=1, source_target_pairs={{0,4},{2,6},{4,0},{6,2},{8,12},{10,14},{12,8},{14,10},{16,20},{18,... | collective-permute-start | bytes 1400840 | tf_op jit(solution)/shard_map/ppermute | solution.py:203
  278.0 21.6 %collective-permute-start.22 = (bf16[192,3072]{1,0:T(8,128)(2,1)S(1)}, bf16[192,3072]{1,0:T(8,128)(2,1)S(1)}, u32[]{:S(2)}, u32[]{:S(2)}) collective-permute-start(bf16[192,3072]{1,0:T(8,128)(2,1)S(1)} %fusion.3), channel_id=1, source_target_pairs={{0,1},{1,0},{2,3},{3,2},{4,5},{5,4},{6,7},{7,6},{8,9},{9,8},{10,11... | collective-permute-start | bytes 3538952 | tf_op jit(solution)/shard_map/ppermute | solution.py:203
  285.2 39.7 %collective-permute-start.31 = (bf16[768,768]{1,0:T(8,128)(2,1)S(1)}, bf16[768,768]{1,0:T(8,128)(2,1)S(1)}, u32[]{:S(2)}, u32[]{:S(2)}) collective-permute-start(bf16[768,768]{1,0:T(8,128)(2,1)S(1)} %fusion.4), channel_id=1, source_target_pairs={{0,1},{1,0},{2,3},{3,2},{4,5},{5,4},{6,7},{7,6},{8,9},{9,8},{10,11... | collective-permute-start | bytes 3538952 | tf_op jit(solution)/shard_map/ppermute | solution.py:203
  287.2 37.9 %collective-permute-start.7 = (bf16[48,1216]{1,0:T(8,128)(2,1)S(1)}, bf16[48,1216]{1,0:T(8,128)(2,1)S(1)}, u32[]{:S(2)}, u32[]{:S(2)}) collective-permute-start(bf16[48,1216]{1,0:T(8,128)(2,1)S(1)} %dynamic-slice_convert_fusion.13), channel_id=1, source_target_pairs={{0,16},{2,18},{4,20},{6,22},{8,24},{10,26},{12,28},{14,30},{16,0},... | collective-permute-start | bytes 350216 | tf_op jit(solution)/shard_map/ppermute | solution.py:203
  300.0 40.5 %collective-permute-start.23 = (bf16[96,3072]{1,0:T(8,128)(2,1)S(1)}, bf16[96,3072]{1,0:T(8,128)(2,1)}, u32[]{:S(2)}, u32[]{:S(2)}) collective-permute-start(bf16[96,3072]{1,0:T(8,128)(2,1)S(1)} %dynamic-slice_convert_fusion.4), channel_id=1, source_target_pairs={{0,4},{2,6},{4,0},{6,2},{8,12},{10,14},{12,8},{14,10},{16,20},{18,... | collective-permute-start | bytes 1769480 | tf_op jit(solution)/shard_map/ppermute | solution.py:203
  325.3 6.0 %collective-permute-start.8 = (bf16[48,1216]{1,0:T(8,128)(2,1)S(1)}, bf16[48,1216]{1,0:T(8,128)(2,1)S(1)}, u32[]{:S(2)}, u32[]{:S(2)}) collective-permute-start(bf16[48,1216]{1,0:T(8,128)(2,1)S(1)} %add_convert_fusion.3), channel_id=1, source_target_pairs={{0,16},{2,18},{4,20},{6,22},{8,24},{10,26},{12,28},{14,30},{16,0},... | collective-permute-start | bytes 350216 | tf_op jit(solution)/shard_map/ppermute | solution.py:203
  327.4 14.5 %collective-permute-start.32 = (bf16[384,768]{1,0:T(8,128)(2,1)}, bf16[384,768]{1,0:T(8,128)(2,1)}, u32[]{:S(2)}, u32[]{:S(2)}) collective-permute-start(bf16[384,768]{1,0:T(8,128)(2,1)} %dynamic-slice_convert_fusion.3), channel_id=1, source_target_pairs={{0,4},{2,6},{4,0},{6,2},{8,12},{10,14},{12,8},{14,10},{16,20},{18,... | collective-permute-start | bytes 1769480 | tf_op jit(solution)/shard_map/ppermute | solution.py:203
  332.5 6.7 %collective-permute-start.9 = (bf16[48,2432]{1,0:T(8,128)(2,1)S(1)}, bf16[48,2432]{1,0:T(8,128)(2,1)S(1)}, u32[]{:S(2)}, u32[]{:S(2)}) collective-permute-start(bf16[48,2432]{1,0:T(8,128)(2,1)S(1)} %dynamic_update_slice.98), channel_id=1, source_target_pairs={{0,8},{2,10},{4,12},{6,14},{8,0},{10,2},{12,4},{14,6},{16,24},{18,... | collective-permute-start | bytes 700424 | tf_op jit(solution)/shard_map/ppermute | solution.py:203
  339.2 13.6 %collective-permute-start.10 = (bf16[96,2432]{1,0:T(8,128)(2,1)S(1)}, bf16[96,2432]{1,0:T(8,128)(2,1)S(1)}, u32[]{:S(2)}, u32[]{:S(2)}) collective-permute-start(bf16[96,2432]{1,0:T(8,128)(2,1)S(1)} %constant_dynamic-update-slice_fusion.20), channel_id=1, source_target_pairs={{0,4},{2,6},{4,0},{6,2},{8,12},{10,14},{12,8},{14,10},{16,20},{18,... | collective-permute-start | bytes 1400840 | tf_op jit(solution)/shard_map/ppermute | solution.py:203
  341.8 7.3 %collective-permute-start.24 = (bf16[48,3072]{1,0:T(8,128)(2,1)S(1)}, bf16[48,3072]{1,0:T(8,128)(2,1)S(1)}, u32[]{:S(2)}, u32[]{:S(2)}) collective-permute-start(bf16[48,3072]{1,0:T(8,128)(2,1)S(1)} %dynamic-slice_convert_fusion.7), channel_id=1, source_target_pairs={{0,8},{2,10},{4,12},{6,14},{8,0},{10,2},{12,4},{14,6},{16,24},{18,... | collective-permute-start | bytes 884744 | tf_op jit(solution)/shard_map/ppermute | solution.py:203
  343.4 9.2 %collective-permute-start.33 = (bf16[192,768]{1,0:T(8,128)(2,1)S(1)}, bf16[192,768]{1,0:T(8,128)(2,1)S(1)}, u32[]{:S(2)}, u32[]{:S(2)}) collective-permute-start(bf16[192,768]{1,0:T(8,128)(2,1)S(1)} %dynamic-slice_convert_fusion.6), channel_id=1, source_target_pairs={{0,8},{2,10},{4,12},{6,14},{8,0},{10,2},{12,4},{14,6},{16,24},{18,... | collective-permute-start | bytes 884744 | tf_op jit(solution)/shard_map/ppermute | solution.py:203
  349.3 15.5 %collective-permute-start.25 = (bf16[48,1536]{1,0:T(8,128)(2,1)S(1)}, bf16[48,1536]{1,0:T(8,128)(2,1)S(1)}, u32[]{:S(2)}, u32[]{:S(2)}) collective-permute-start(bf16[48,1536]{1,0:T(8,128)(2,1)S(1)} %dynamic-slice_convert_fusion.11), channel_id=1, source_target_pairs={{0,16},{2,18},{4,20},{6,22},{8,24},{10,26},{12,28},{14,30},{16,0},... | collective-permute-start | bytes 442376 | tf_op jit(solution)/shard_map/ppermute | solution.py:203
  352.7 14.3 %collective-permute-start.34 = (bf16[96,768]{1,0:T(8,128)(2,1)S(1)}, bf16[96,768]{1,0:T(8,128)(2,1)S(1)}, u32[]{:S(2)}, u32[]{:S(2)}) collective-permute-start(bf16[96,768]{1,0:T(8,128)(2,1)S(1)} %dynamic-slice_convert_fusion.10), channel_id=1, source_target_pairs={{0,16},{2,18},{4,20},{6,22},{8,24},{10,26},{12,28},{14,30},{16,0},... | collective-permute-start | bytes 442376 | tf_op jit(solution)/shard_map/ppermute | solution.py:203
  352.9 55.0 %collective-permute-start.11 = (bf16[192,2432]{1,0:T(8,128)(2,1)S(1)}, bf16[192,2432]{1,0:T(8,128)(2,1)S(1)}, u32[]{:S(2)}, u32[]{:S(2)}) collective-permute-start(bf16[192,2432]{1,0:T(8,128)(2,1)S(1)} %constant_dynamic-update-slice_fusion.18), channel_id=1, source_target_pairs={{0,2},{2,0},{4,6},{6,4},{8,10},{10,8},{12,14},{14,12},{16,18},{18,... | collective-permute-start | bytes 2801672 | tf_op jit(solution)/shard_map/ppermute | solution.py:203
  364.8 11.8 %collective-permute-start.26 = (bf16[48,1536]{1,0:T(8,128)(2,1)S(1)}, bf16[48,1536]{1,0:T(8,128)(2,1)S(1)}, u32[]{:S(2)}, u32[]{:S(2)}) collective-permute-start(bf16[48,1536]{1,0:T(8,128)(2,1)S(1)} %get-tuple-element.72), channel_id=1, source_target_pairs={{0,16},{2,18},{4,20},{6,22},{8,24},{10,26},{12,28},{14,30},{16,0},... | collective-permute-start | bytes 442376 | tf_op jit(solution)/shard_map/ppermute | solution.py:203
  367.1 14.4 %collective-permute-start.35 = (bf16[96,768]{1,0:T(8,128)(2,1)S(1)}, bf16[96,768]{1,0:T(8,128)(2,1)S(1)}, u32[]{:S(2)}, u32[]{:S(2)}) collective-permute-start(bf16[96,768]{1,0:T(8,128)(2,1)S(1)} %get-tuple-element.70), channel_id=1, source_target_pairs={{0,16},{2,18},{4,20},{6,22},{8,24},{10,26},{12,28},{14,30},{16,0},... | collective-permute-start | bytes 442376 | tf_op jit(solution)/shard_map/ppermute | solution.py:203
  376.7 8.6 %collective-permute-start.27 = (bf16[48,3072]{1,0:T(8,128)(2,1)S(1)}, bf16[48,3072]{1,0:T(8,128)(2,1)S(1)}, u32[]{:S(2)}, u32[]{:S(2)}) collective-permute-start(bf16[48,3072]{1,0:T(8,128)(2,1)S(1)} %constant_dynamic-update-slice_fusion.10), channel_id=1, source_target_pairs={{0,8},{2,10},{4,12},{6,14},{8,0},{10,2},{12,4},{14,6},{16,24},{18,... | collective-permute-start | bytes 884744 | tf_op jit(solution)/shard_map/ppermute | solution.py:203
  381.5 10.1 %collective-permute-start.36 = (bf16[192,768]{1,0:T(8,128)(2,1)S(1)}, bf16[192,768]{1,0:T(8,128)(2,1)S(1)}, u32[]{:S(2)}, u32[]{:S(2)}) collective-permute-start(bf16[192,768]{1,0:T(8,128)(2,1)S(1)} %constant_dynamic-update-slice_fusion.4), channel_id=1, source_target_pairs={{0,8},{2,10},{4,12},{6,14},{8,0},{10,2},{12,4},{14,6},{16,24},{18,... | collective-permute-start | bytes 884744 | tf_op jit(solution)/shard_map/ppermute | solution.py:203
  385.3 11.1 %collective-permute-start.28 = (bf16[96,3072]{1,0:T(8,128)(2,1)S(1)}, bf16[96,3072]{1,0:T(8,128)(2,1)S(1)}, u32[]{:S(2)}, u32[]{:S(2)}) collective-permute-start(bf16[96,3072]{1,0:T(8,128)(2,1)S(1)} %constant_dynamic-update-slice_fusion.8), channel_id=1, source_target_pairs={{0,4},{2,6},{4,0},{6,2},{8,12},{10,14},{12,8},{14,10},{16,20},{18,... | collective-permute-start | bytes 1769480 | tf_op jit(solution)/shard_map/ppermute | solution.py:203
  392.3 21.0 %collective-permute-start.37 = (bf16[384,768]{1,0:T(8,128)(2,1)}, bf16[384,768]{1,0:T(8,128)(2,1)}, u32[]{:S(2)}, u32[]{:S(2)}) collective-permute-start(bf16[384,768]{1,0:T(8,128)(2,1)} %constant_dynamic-update-slice_fusion.2), channel_id=1, source_target_pairs={{0,4},{2,6},{4,0},{6,2},{8,12},{10,14},{12,8},{14,10},{16,20},{18,... | collective-permute-start | bytes 1769480 | tf_op jit(solution)/shard_map/ppermute | solution.py:203
  396.5 19.8 %collective-permute-start.29 = (bf16[192,3072]{1,0:T(8,128)(2,1)S(1)}, bf16[192,3072]{1,0:T(8,128)(2,1)}, u32[]{:S(2)}, u32[]{:S(2)}) collective-permute-start(bf16[192,3072]{1,0:T(8,128)(2,1)S(1)} %constant_dynamic-update-slice_fusion.6), channel_id=1, source_target_pairs={{0,2},{2,0},{4,6},{6,4},{8,10},{10,8},{12,14},{14,12},{16,18},{18,... | collective-permute-start | bytes 3538952 | tf_op jit(solution)/shard_map/ppermute | solution.py:203
  414.5 5.9 %collective-permute-start.38 = (bf16[768,768]{1,0:T(8,128)(2,1)S(1)}, bf16[768,768]{1,0:T(8,128)(2,1)S(1)}, u32[]{:S(2)}, u32[]{:S(2)}) collective-permute-start(bf16[768,768]{1,0:T(8,128)(2,1)S(1)} %constant_dynamic-update-slice_fusion), channel_id=1, source_target_pairs={{0,2},{2,0},{4,6},{6,4},{8,10},{10,8},{12,14},{14,12},{16,18},{18,... | collective-permute-start | bytes 3538952 | tf_op jit(solution)/shard_map/ppermute | solution.py:203
  (46 other events, 395.1 us)
